TPU v7x, 32 devices: a whole 2x2x4 slice. The times are simulated.
32 devices in a mesh: fsdp: 16 (over z, y, core), seq: 2 (over x).
Axes of the slice: x: 2, y: 2, z: 4, core: 2. Of those that a mesh axis runs over, the one named last changes fastest.
Arguments:
- hidden: bfloat16 [32, 1024, 768], P('fsdp', 'seq'), may hold values from -6 to 6
- segments: int32 [32, 1024], P('fsdp'), may hold values from 0 to 7, never falling along the last dimension, each value on 1 to 512 neighbouring positions
- block_perm: int32 [12, 2], replicated, may hold values from 0 to 1, each once within a row
- query_weight: bfloat16 [768, 768], P('fsdp'), may hold values from -0.21875 to 0.21875
- query_bias: bfloat16 [768], P('fsdp'), may hold values from -3 to 3
- key_weight: bfloat16 [768, 768], P('fsdp'), may hold values from -0.21875 to 0.21875
- value_weight: bfloat16 [768, 768], P('fsdp'), may hold values from -0.21875 to 0.21875
- value_bias: bfloat16 [768], P('fsdp'), may hold values from -3 to 3
- output_weight: bfloat16 [768, 768], P('fsdp'), may hold values from -0.875 to 0.875
- output_bias: bfloat16 [768], P('fsdp'), may hold values from -3 to 3
- first_gain: bfloat16 [768], P('fsdp'), may hold values from 0.5 to 1.5
- first_shift: bfloat16 [768], P('fsdp'), may hold values from -3 to 3
- inner_weight: bfloat16 [768, 3072], P('fsdp'), may hold values from -0.21875 to 0.21875
- inner_bias: bfloat16 [3072], P('fsdp'), may hold values from -3 to 3
- outer_weight: bfloat16 [3072, 768], P('fsdp'), may hold values from -0.109375 to 0.109375
- outer_bias: bfloat16 [768], P('fsdp'), may hold values from -3 to 3
- second_gain: bfloat16 [768], P('fsdp'), may hold values from 0.5 to 1.5
- second_shift: bfloat16 [768], P('fsdp'), may hold values from -3 to 3
- cotangent: bfloat16 [32, 1024, 768], P('fsdp', 'seq'), may hold values from -6 to 6
Outputs:
- layer_out: bfloat16 [32, 1024, 768], P('fsdp', 'seq')
- hidden_grad: bfloat16 [32, 1024, 768], P('fsdp', 'seq')
- query_weight_grad: float32 [768, 768], P('fsdp')
- query_bias_grad: float32 [768], P('fsdp')
- key_weight_grad: float32 [768, 768], P('fsdp')
- value_weight_grad: float32 [768, 768], P('fsdp')
- value_bias_grad: float32 [768], P('fsdp')
- output_weight_grad: float32 [768, 768], P('fsdp')
- output_bias_grad: float32 [768], P('fsdp')
- first_gain_grad: float32 [768], P('fsdp')
- first_shift_grad: float32 [768], P('fsdp')
- inner_weight_grad: float32 [768, 3072], P('fsdp')
- inner_bias_grad: float32 [3072], P('fsdp')
- outer_weight_grad: float32 [3072, 768], P('fsdp')
- outer_bias_grad: float32 [768], P('fsdp')
- second_gain_grad: float32 [768], P('fsdp')
- second_shift_grad: float32 [768], P('fsdp')
Inputs may be any that keep to these rules, and one draw needn't show every extreme that they name: `segments`: segment numbers never fall along a sequence; each document spans at most 512 tokens and one spans exactly that many. `block_perm`: each row names each of the 2 blocks once.
All inputs are finite; a program needn't handle non-finite values.
Results may differ from a plain program's by a relative error of at most 0.015.
Values may be sent and summed in bfloat16 or wider, within the bound.
No kernel may reach another device: no remote copies, remote signals or barrier semaphores. Data moves between devices by JAX's collectives and lax.ppermute only.
A program may use at most 192 MiB of HBM per device.

v0:
```python
import jax
import jax.numpy as jnp
from jax import lax
from jax.sharding import PartitionSpec as P

H = 12
HD = 64


EPSILON = 1e-05


def shortened(array):
    return jax.tree.map(lambda a: a.astype(jnp.bfloat16) if a.dtype == jnp.float32 else a, array)


def norm_core(values, gain):
    average = jnp.mean(values, axis=-1, keepdims=True)
    centered = values - average
    spread = jnp.mean(centered * centered, axis=-1, keepdims=True)
    return centered * lax.rsqrt(spread + EPSILON) * gain


def exact_gelu(values):
    return jax.nn.gelu(values, approximate=False)


def matmul(left, right):
    return jnp.dot(left, right, preferred_element_type=jnp.float32)


def times_transposed(left, right):
    return lax.dot_general(
        left, right, (((1,), (1,)), ((), ())), preferred_element_type=jnp.float32
    )


def transposed_times(left, right):
    return lax.dot_general(
        left, right, (((0,), (0,)), ((), ())), preferred_element_type=jnp.float32
    )


def column_sum(values):
    return jnp.sum(values.astype(jnp.float32), axis=0)


def select_blocks(blocked, target):
    return jnp.take_along_axis(blocked, target[:, None, None, None], axis=1)[:, 0]


def block_scores(query_block, chosen_keys, query_segments, key_segments, scale):
    scores = (
        jnp.einsum("qhd,hkd->hqk", query_block, chosen_keys, preferred_element_type=jnp.float32)
        * scale
    )
    same_doc = query_segments[None, :, None] == key_segments[:, None, :]
    mirror = lax.broadcasted_iota(jnp.int32, scores.shape, 1) == lax.broadcasted_iota(
        jnp.int32, scores.shape, 2
    )
    return jnp.where(same_doc | mirror, scores, -1e30)


def split_layout(query_all, keys_all, values_all, segment_row, perm_local, head_dim):
    length, width = query_all.shape
    heads = width // head_dim
    block_count = perm_local.shape[1]
    block_rows = length // block_count
    shaped = (block_count, block_rows, heads, head_dim)
    query_split = query_all.reshape(shaped)
    keys_split = keys_all.reshape(shaped).transpose(2, 0, 1, 3)
    values_split = values_all.reshape(shaped).transpose(2, 0, 1, 3)
    segment_split = segment_row.reshape(block_count, block_rows)
    return (query_split, keys_split, values_split, segment_split, shaped)


def attend_forward(query_all, keys_all, values_all, segment_row, perm_local, head_dim):
    length, width = query_all.shape
    query_split, keys_split, values_split, segment_split, shaped = split_layout(
        query_all, keys_all, values_all, segment_row, perm_local, head_dim
    )
    scale = head_dim ** (-0.5)
    contexts = []
    log_totals = []
    for block in range(shaped[0]):
        target = perm_local[:, block]
        chosen_keys = select_blocks(keys_split, target)
        chosen_values = select_blocks(values_split, target)
        masked = block_scores(
            query_split[block], chosen_keys, segment_split[block], segment_split[target], scale
        )
        row_max = jnp.max(masked, axis=-1, keepdims=True)
        lifted = jnp.exp(masked - row_max)
        total = jnp.sum(lifted, axis=-1, keepdims=True)
        probs = (lifted / total).astype(jnp.bfloat16)
        piece = jnp.einsum("hqk,hkd->qhd", probs, chosen_values, preferred_element_type=jnp.float32)
        contexts.append(piece.astype(jnp.bfloat16))
        log_totals.append(row_max + jnp.log(total))
    return (jnp.concatenate(contexts, axis=0).reshape(length, width), jnp.stack(log_totals))


def attend_backward(
    query_all, keys_all, values_all, slope_all, segment_row, perm_local, log_totals, head_dim
):
    length, width = query_all.shape
    query_split, keys_split, values_split, segment_split, shaped = split_layout(
        query_all, keys_all, values_all, segment_row, perm_local, head_dim
    )
    block_count, block_rows, heads = (shaped[0], shaped[1], shaped[2])
    slope_split = slope_all.reshape(shaped)
    scale = head_dim ** (-0.5)
    key_slots = jnp.zeros((heads, block_count, block_rows, head_dim), jnp.float32)
    value_slots = jnp.zeros((heads, block_count, block_rows, head_dim), jnp.float32)
    block_ids = jnp.arange(block_count, dtype=jnp.int32)
    query_slopes = []
    for block in range(block_count):
        target = perm_local[:, block]
        chosen_keys = select_blocks(keys_split, target)
        chosen_values = select_blocks(values_split, target)
        masked = block_scores(
            query_split[block], chosen_keys, segment_split[block], segment_split[target], scale
        )
        probs = jnp.exp(masked - log_totals[block])
        slope_probs = jnp.einsum(
            "qhd,hkd->hqk", slope_split[block], chosen_values, preferred_element_type=jnp.float32
        )
        row_dot = jnp.sum(probs * slope_probs, axis=-1, keepdims=True)
        slope_scores = (probs * (slope_probs - row_dot)).astype(jnp.bfloat16)
        query_part = (
            jnp.einsum(
                "hqk,hkd->qhd", slope_scores, chosen_keys, preferred_element_type=jnp.float32
            )
            * scale
        )
        query_slopes.append(query_part.astype(jnp.bfloat16))
        key_part = (
            jnp.einsum(
                "hqk,qhd->hkd", slope_scores, query_split[block], preferred_element_type=jnp.float32
            )
            * scale
        )
        value_part = jnp.einsum(
            "hqk,qhd->hkd",
            probs.astype(jnp.bfloat16),
            slope_split[block],
            preferred_element_type=jnp.float32,
        )
        hit = (target[:, None] == block_ids[None, :])[:, :, None, None]
        key_slots = jnp.where(hit, key_part[:, None], key_slots)
        value_slots = jnp.where(hit, value_part[:, None], value_slots)
    slope_query = jnp.concatenate(query_slopes, axis=0).reshape(length, width)
    slope_keys = key_slots.transpose(1, 2, 0, 3).reshape(length, width).astype(jnp.bfloat16)
    slope_values = value_slots.transpose(1, 2, 0, 3).reshape(length, width).astype(jnp.bfloat16)
    return (slope_query, slope_keys, slope_values)


def on_device(
    hidden,
    segments,
    block_perm,
    query_weight,
    query_bias,
    key_weight,
    value_weight,
    value_bias,
    output_weight,
    output_bias,
    first_gain,
    first_shift,
    inner_weight,
    inner_bias,
    outer_weight,
    outer_bias,
    second_gain,
    second_shift,
    cotangent,
):
    micro = hidden.shape[0]
    heads_here = H // lax.axis_size("seq")
    perm_local = lax.dynamic_slice_in_dim(
        block_perm, lax.axis_index("seq") * heads_here, heads_here, 0
    )
    shards = (
        query_weight,
        query_bias,
        key_weight,
        value_weight,
        value_bias,
        output_weight,
        output_bias,
        first_gain,
        first_shift,
        inner_weight,
        inner_bias,
        outer_weight,
        outer_bias,
        second_gain,
        second_shift,
    )
    matrices = (
        query_weight,
        key_weight,
        value_weight,
        output_weight,
        inner_weight,
        outer_weight,
        first_gain,
        second_gain,
    )
    sums = tuple(
        (
            jnp.zeros((piece.shape[0] * lax.axis_size("fsdp"),) + piece.shape[1:], jnp.float32)
            for piece in shards
        )
    )
    f32 = jnp.float32
    bf16 = jnp.bfloat16

    def one_batch(index, carry):
        layer_out, hidden_grad, totals = carry
        rows = lax.dynamic_index_in_dim(hidden, index, 0, keepdims=False)
        segment_row = lax.dynamic_index_in_dim(segments, index, 0, keepdims=False)
        grad_out = lax.dynamic_index_in_dim(cotangent, index, 0, keepdims=False).astype(f32)
        ahead = (
            lax.all_gather(shards[0], "fsdp", axis=0, tiled=True),
            lax.all_gather(shards[1], "fsdp", axis=0, tiled=True),
            lax.all_gather(shards[2], "fsdp", axis=0, tiled=True),
            lax.all_gather(shards[3], "fsdp", axis=0, tiled=True),
            lax.all_gather(shards[4], "fsdp", axis=0, tiled=True),
            lax.all_gather(shards[5], "fsdp", axis=0, tiled=True),
            lax.all_gather(shards[6], "fsdp", axis=0, tiled=True),
            lax.all_gather(shards[7], "fsdp", axis=0, tiled=True),
            lax.all_gather(shards[8], "fsdp", axis=0, tiled=True),
            lax.all_gather(shards[9], "fsdp", axis=0, tiled=True),
            lax.all_gather(shards[10], "fsdp", axis=0, tiled=True),
            lax.all_gather(shards[11], "fsdp", axis=0, tiled=True),
            lax.all_gather(shards[12], "fsdp", axis=0, tiled=True),
            lax.all_gather(shards[13], "fsdp", axis=0, tiled=True),
            lax.all_gather(shards[14], "fsdp", axis=0, tiled=True),
        )
        (
            whole_query,
            query_shift,
            whole_key,
            whole_value,
            value_shift,
            whole_output,
            output_shift,
            gain_one,
            shift_one,
            whole_inner,
            inner_shift,
            whole_outer,
            outer_shift,
            gain_two,
            shift_two,
        ) = ahead
        query = (matmul(rows, whole_query) + query_shift.astype(f32)).astype(bf16)
        keys = matmul(rows, whole_key).astype(bf16)
        values = (matmul(rows, whole_value) + value_shift.astype(f32)).astype(bf16)
        query_all, keys_all, values_all = (
            lax.all_to_all(query, "seq", split_axis=1, concat_axis=0, tiled=True),
            lax.all_to_all(keys, "seq", split_axis=1, concat_axis=0, tiled=True),
            lax.all_to_all(values, "seq", split_axis=1, concat_axis=0, tiled=True),
        )
        context, log_totals = attend_forward(
            query_all, keys_all, values_all, segment_row, perm_local, HD
        )
        context_rows = lax.all_to_all(
            shortened(context), "seq", split_axis=0, concat_axis=1, tiled=True
        ).astype(context.dtype)
        first = rows.astype(f32) + (matmul(context_rows, whole_output) + output_shift.astype(f32))
        normed = norm_core(first, gain_one.astype(f32)) + shift_one.astype(f32)
        normed_low = normed.astype(bf16)
        inner = matmul(normed_low, whole_inner) + inner_shift.astype(f32)
        active = exact_gelu(inner).astype(bf16)
        second = normed + (matmul(active, whole_outer) + outer_shift.astype(f32))
        result = norm_core(second, gain_two.astype(f32)) + shift_two.astype(f32)
        behind = (
            lax.all_gather(matrices[0], "fsdp", axis=0, tiled=True),
            lax.all_gather(matrices[1], "fsdp", axis=0, tiled=True),
            lax.all_gather(matrices[2], "fsdp", axis=0, tiled=True),
            lax.all_gather(matrices[3], "fsdp", axis=0, tiled=True),
            lax.all_gather(matrices[4], "fsdp", axis=0, tiled=True),
            lax.all_gather(matrices[5], "fsdp", axis=0, tiled=True),
            lax.all_gather(matrices[6], "fsdp", axis=0, tiled=True),
            lax.all_gather(matrices[7], "fsdp", axis=0, tiled=True),
        )
        (
            back_query,
            back_key,
            back_value,
            back_output,
            back_inner,
            back_outer,
            back_gain_one,
            back_gain_two,
        ) = behind
        _, second_back = jax.vjp(norm_core, second, back_gain_two.astype(f32))
        slope_second, grad_gain_two = second_back(grad_out)
        grad_shift_two = jnp.sum(grad_out, axis=0)
        slope_outer = slope_second.astype(bf16)
        grad_outer_shift = column_sum(slope_outer)
        grad_outer = transposed_times(active, slope_outer)
        _, gelu_back = jax.vjp(exact_gelu, inner)
        slope_inner = gelu_back(times_transposed(slope_outer, back_outer))[0].astype(bf16)
        grad_inner_shift = column_sum(slope_inner)
        grad_inner = transposed_times(normed_low, slope_inner)
        slope_normed = slope_second + times_transposed(slope_inner, back_inner)
        _, first_back = jax.vjp(norm_core, first, back_gain_one.astype(f32))
        slope_first, grad_gain_one = first_back(slope_normed)
        grad_shift_one = jnp.sum(slope_normed, axis=0)
        slope_attn = slope_first.astype(bf16)
        grad_output_shift = column_sum(slope_attn)
        grad_output = transposed_times(context_rows, slope_attn)
        slope_context = times_transposed(slope_attn, back_output).astype(bf16)
        slope_context_all = lax.all_to_all(
            slope_context, "seq", split_axis=1, concat_axis=0, tiled=True
        )
        slope_query_all, slope_keys_all, slope_values_all = attend_backward(
            query_all,
            keys_all,
            values_all,
            slope_context_all,
            segment_row,
            perm_local,
            log_totals,
            HD,
        )
        slope_query, slope_keys, slope_values = (
            lax.all_to_all(
                shortened(slope_query_all), "seq", split_axis=0, concat_axis=1, tiled=True
            ).astype(slope_query_all.dtype),
            lax.all_to_all(slope_keys_all, "seq", split_axis=0, concat_axis=1, tiled=True),
            lax.all_to_all(slope_values_all, "seq", split_axis=0, concat_axis=1, tiled=True),
        )
        grad_query = transposed_times(rows, slope_query)
        grad_query_shift = column_sum(slope_query)
        grad_key = transposed_times(rows, slope_keys)
        grad_value = transposed_times(rows, slope_values)
        grad_value_shift = column_sum(slope_values)
        slope_rows = (
            slope_first
            + times_transposed(slope_query, back_query)
            + times_transposed(slope_keys, back_key)
            + times_transposed(slope_values, back_value)
        )
        grads = (
            grad_query,
            grad_query_shift,
            grad_key,
            grad_value,
            grad_value_shift,
            grad_output,
            grad_output_shift,
            grad_gain_one,
            grad_shift_one,
            grad_inner,
            grad_inner_shift,
            grad_outer,
            grad_outer_shift,
            grad_gain_two,
            grad_shift_two,
        )
        totals = jax.tree.map(lambda total, piece: total + piece, totals, grads)
        layer_out = lax.dynamic_update_index_in_dim(layer_out, result.astype(bf16), index, 0)
        hidden_grad = lax.dynamic_update_index_in_dim(
            hidden_grad, slope_rows.astype(bf16), index, 0
        )
        return (layer_out, hidden_grad, totals)

    start = (jnp.zeros(hidden.shape, bf16), jnp.zeros(hidden.shape, bf16), sums)
    layer_out, hidden_grad, sums = lax.fori_loop(0, micro, one_batch, start)
    owned = lax.psum_scatter(sums, "fsdp", scatter_dimension=0, tiled=True)
    sums = jax.tree.map(lambda part: part.astype(jnp.float32), lax.psum(shortened(owned), "seq"))
    return (layer_out, hidden_grad) + tuple(sums)


def solution(mesh):
    in_specs = (
        P("fsdp", "seq", None),
        P("fsdp", None),
        P(),
        P("fsdp", None),
        P("fsdp"),
        P("fsdp", None),
        P("fsdp", None),
        P("fsdp"),
        P("fsdp", None),
        P("fsdp"),
        P("fsdp"),
        P("fsdp"),
        P("fsdp", None),
        P("fsdp"),
        P("fsdp", None),
        P("fsdp"),
        P("fsdp"),
        P("fsdp"),
        P("fsdp", "seq", None),
    )
    out_specs = (
        P("fsdp", "seq", None),
        P("fsdp", "seq", None),
        P("fsdp", None),
        P("fsdp"),
        P("fsdp", None),
        P("fsdp", None),
        P("fsdp"),
        P("fsdp", None),
        P("fsdp"),
        P("fsdp"),
        P("fsdp"),
        P("fsdp", None),
        P("fsdp"),
        P("fsdp", None),
        P("fsdp"),
        P("fsdp"),
        P("fsdp"),
    )
    return jax.shard_map(
        on_device, mesh=mesh, in_specs=in_specs, out_specs=out_specs, check_vma=False
    )
```

profile of v0, /device:TPU:0, one launch (start us, length us, event | category | flops | bytes accessed | tf_op | source)
XLA Modules:
  0.0 1410.1 jit_solution(1187282941288854531)
XLA Ops:
  9.3 815.6 %while.46 = (s32[]{:T(128)}, bf16[2,512,768]{2,1,0:T(8,128)(2,1)}, bf16[2,512,768]{2,1,0:T(8,128)(2,1)}, f32[768,768]{1,0:T(8,128)}, f32[768]{0:T(1024)}, /*inde...) while((s32[]{:T(128)}, bf16[2,512,768]{2,1,0:T(8,128)(2,1)}, ...), condition=%wide.region_24.26_spmd.clone, body=%wide.region_0.25_spmd.clone.sunk | while | flops 24410482688 | bytes 680891776 | solution.py:373
  27.5 63.5 %all-reduce.32 = (bf16[768]{0:T(1024)(128)(2,1)S(1)}, bf16[768]{0:T(1024)(128)(2,1)S(1)}, bf16[768]{0:T(1024)(128)(2,1)S(1)}, bf16[768]{0:T(1024)(128)(2,1)S(1)}...) all-reduce(bf16[768]{0:T(1024)(128)(2,1)S(1)} %dynamic-update-slice, ...), channel_id=1, replica_groups=mesh['fsdp'=16,'seq'=2] {'fsdp'}, use_global_device_ids=true, to_apply=%add.1 | all-reduce | flops 9216 | bytes 36864 | tf_op jit(solution)/shard_map/while
  111.6 20.9 %all-gather.13.cloned.1.call-done = bf16[768,768]{1,0:T(8,128)(2,1)} async-done(((bf16[48,768]{1,0:T(8,128)(2,1)}), bf16[768,768]{1,0:T(8,128)(2,1)}) %all-gather.13.cloned.1.call-update) | async-done | bytes 1179664 | tf_op jit(solution)/shard_map/while/body/eval_jaxpr/all_gather | solution.py:228
  148.5 6.0 all-to-all-done.2
  174.4 7.9 all-to-all-done.3
  186.5 39.5 %all-gather.7.cloned.1.call-done = bf16[768,3072]{1,0:T(8,128)(2,1)} async-done(((bf16[48,3072]{1,0:T(8,128)(2,1)}), bf16[768,3072]{1,0:T(8,128)(2,1)}) %all-gather.7.cloned.1.call-update) | async-done | bytes 4718608 | tf_op jit(solution)/shard_map/while/body/eval_jaxpr/all_gather | solution.py:234
  226.0 19.7 %multiply_convert_fusion.6 = (bf16[512,3072]{1,0:T(8,128)(2,1)}, f32[512,3072]{1,0:T(8,128)}, f32[512,3072]{1,0:T(8,128)}) fusion(f32[3072]{0:T(1024)} %convert_element_type.610, bf16[768,3072]{1,0:T(8,128)(2,1)} %all-gather.7.cloned.1.call-done, f32[512,768]{1,0:T(8,128)S(1)} %get-tuple-element.1209, f32[768]{0:T(1024)S(1)} %convert_element_type.614, ...), kind=kOutput, calls=%fused_computation.18.clone.1 | convolution fusion | flops 2521694208 | bytes 22042624 | tf_op jit(solution)/shard_map/while/body/eval_jaxpr/dot_general | solution.py:29
  245.7 34.2 %all-gather.17.cloned.1.call-done = bf16[3072,768]{1,0:T(8,128)(2,1)} async-done(((bf16[192,768]{1,0:T(8,128)(2,1)}), bf16[3072,768]{1,0:T(8,128)(2,1)}) %all-gather.17.cloned.1.call-update) | async-done | bytes 4718608 | tf_op jit(solution)/shard_map/while/body/eval_jaxpr/all_gather | solution.py:236
  279.9 6.2 fusion.279
  290.1 9.0 convert_reduce_fusion.13
  311.5 7.5 select_add_fusion.36
  371.7 7.8 all-to-all-done.7
  384.4 9.2 all-to-all-done.5
  433.3 57.9 %all-reduce.32 = (bf16[768]{0:T(1024)(128)(2,1)S(1)}, bf16[768]{0:T(1024)(128)(2,1)S(1)}, bf16[768]{0:T(1024)(128)(2,1)S(1)}, bf16[768]{0:T(1024)(128)(2,1)S(1)}...) all-reduce(bf16[768]{0:T(1024)(128)(2,1)S(1)} %dynamic-update-slice, ...), channel_id=1, replica_groups=mesh['fsdp'=16,'seq'=2] {'fsdp'}, use_global_device_ids=true, to_apply=%add.1 | all-reduce | flops 9216 | bytes 36864 | tf_op jit(solution)/shard_map/while
  511.9 21.2 %all-gather.13.cloned.1.call-done = bf16[768,768]{1,0:T(8,128)(2,1)} async-done(((bf16[48,768]{1,0:T(8,128)(2,1)}), bf16[768,768]{1,0:T(8,128)(2,1)}) %all-gather.13.cloned.1.call-update) | async-done | bytes 1179664 | tf_op jit(solution)/shard_map/while/body/eval_jaxpr/all_gather | solution.py:228
  574.8 7.8 all-to-all-done.3
  587.0 39.8 %all-gather.7.cloned.1.call-done = bf16[768,3072]{1,0:T(8,128)(2,1)} async-done(((bf16[48,3072]{1,0:T(8,128)(2,1)}), bf16[768,3072]{1,0:T(8,128)(2,1)}) %all-gather.7.cloned.1.call-update) | async-done | bytes 4718608 | tf_op jit(solution)/shard_map/while/body/eval_jaxpr/all_gather | solution.py:234
  626.7 19.7 %multiply_convert_fusion.6 = (bf16[512,3072]{1,0:T(8,128)(2,1)}, f32[512,3072]{1,0:T(8,128)}, f32[512,3072]{1,0:T(8,128)}) fusion(f32[3072]{0:T(1024)} %convert_element_type.610, bf16[768,3072]{1,0:T(8,128)(2,1)} %all-gather.7.cloned.1.call-done, f32[512,768]{1,0:T(8,128)S(1)} %get-tuple-element.1209, f32[768]{0:T(1024)S(1)} %convert_element_type.614, ...), kind=kOutput, calls=%fused_computation.18.clone.1 | convolution fusion | flops 2521694208 | bytes 22042624 | tf_op jit(solution)/shard_map/while/body/eval_jaxpr/dot_general | solution.py:29
  646.4 34.2 %all-gather.17.cloned.1.call-done = bf16[3072,768]{1,0:T(8,128)(2,1)} async-done(((bf16[192,768]{1,0:T(8,128)(2,1)}), bf16[3072,768]{1,0:T(8,128)(2,1)}) %all-gather.17.cloned.1.call-update) | async-done | bytes 4718608 | tf_op jit(solution)/shard_map/while/body/eval_jaxpr/all_gather | solution.py:236
  680.6 6.2 fusion.279
  690.8 8.9 convert_reduce_fusion.13
  712.2 8.9 select_add_fusion.36
  721.2 7.7 select_add_fusion.38
  777.7 7.8 all-to-all-done.7
  790.5 9.2 all-to-all-done.5
  829.1 61.3 %reduce-scatter.7.cloned.1.call-done = f32[48,768]{1,0:T(8,128)} async-done(((f32[768,768]{1,0:T(8,128)}), f32[48,768]{1,0:T(8,128)}) %reduce-scatter.7.cloned.1.call-update) | async-done | bytes 147472 | tf_op jit(solution)/shard_map/reduce_scatter | solution.py:374
  891.9 64.5 %reduce-scatter.9.cloned.1.call-done = f32[48,768]{1,0:T(8,128)} async-done(((f32[768,768]{1,0:T(8,128)}), f32[48,768]{1,0:T(8,128)}) %reduce-scatter.9.cloned.1.call-update) | async-done | bytes 147472 | tf_op jit(solution)/shard_map/reduce_scatter | solution.py:374
  958.0 64.5 %reduce-scatter.11.cloned.1.call-done = f32[48,768]{1,0:T(8,128)} async-done(((f32[768,768]{1,0:T(8,128)}), f32[48,768]{1,0:T(8,128)}) %reduce-scatter.11.cloned.1.call-update) | async-done | bytes 147472 | tf_op jit(solution)/shard_map/reduce_scatter | solution.py:374
  1024.0 64.7 %reduce-scatter.13.cloned.1.call-done = f32[48,768]{1,0:T(8,128)} async-done(((f32[768,768]{1,0:T(8,128)}), f32[48,768]{1,0:T(8,128)}) %reduce-scatter.13.cloned.1.call-update) | async-done | bytes 147472 | tf_op jit(solution)/shard_map/reduce_scatter | solution.py:374
  1090.3 112.8 %reduce-scatter.15.cloned.1.call-done = f32[48,3072]{1,0:T(8,128)} async-done(((f32[768,3072]{1,0:T(8,128)}), f32[48,3072]{1,0:T(8,128)}) %reduce-scatter.15.cloned.1.call-update) | async-done | bytes 589840 | tf_op jit(solution)/shard_map/reduce_scatter | solution.py:374
  1204.9 113.1 %reduce-scatter.17.cloned.1.call-done = f32[192,768]{1,0:T(8,128)} async-done(((f32[3072,768]{1,0:T(8,128)}), f32[192,768]{1,0:T(8,128)}) %reduce-scatter.17.cloned.1.call-update) | async-done | bytes 589840 | tf_op jit(solution)/shard_map/reduce_scatter | solution.py:374
  1321.9 60.3 %all-reduce.28 = (bf16[768]{0:T(1024)(128)(2,1)S(1)}, bf16[768]{0:T(1024)(128)(2,1)S(1)}, bf16[768]{0:T(1024)(128)(2,1)S(1)}, bf16[768]{0:T(1024)(128)(2,1)S(1)}...) all-reduce(f32[768]{0:T(1024)S(1)} %copy-done.85, ...), channel_id=3, replica_groups=mesh['fsdp'=16,'seq'=2] {'fsdp'}, use_global_device_ids=true, to_apply=%region_27.29.clone | all-reduce | flops 9216 | bytes 55296
  (813 shorter events, 382.2 us)
Async XLA Ops:
  9.3 81.7 %all-gather.9.cloned.1.call-start = ((), (), s32[]{:S(2)}) async-start(), calls=%async_computation.22 | async-start | bytes 1253376 | tf_op jit(solution)/shard_map/while/body/eval_jaxpr/all_gather | solution.py:225
  10.1 94.8 %all-gather.11.cloned.1.call-start = ((), (), s32[]{:S(2)}) async-start(), calls=%async_computation.23 | async-start | bytes 1253376 | tf_op jit(solution)/shard_map/while/body/eval_jaxpr/all_gather | solution.py:227
  10.8 121.7 %all-gather.13.cloned.1.call-start = ((), (), s32[]{:S(2)}) async-start(), calls=%async_computation.24 | async-start | bytes 1253376 | tf_op jit(solution)/shard_map/while/body/eval_jaxpr/all_gather | solution.py:228
  11.6 162.8 %all-gather.15.cloned.1.call-start = ((), (), s32[]{:S(2)}) async-start(), calls=%async_computation.25 | async-start | bytes 1253376 | tf_op jit(solution)/shard_map/while/body/eval_jaxpr/all_gather | solution.py:230
  12.1 213.9 %all-gather.7.cloned.1.call-start = ((), (), s32[]{:S(2)}) async-start(), calls=%async_computation.21 | async-start | bytes 5013504 | tf_op jit(solution)/shard_map/while/body/eval_jaxpr/all_gather | solution.py:234
  12.7 267.2 %all-gather.17.cloned.1.call-start = ((), (), s32[]{:S(2)}) async-start(), calls=%async_computation.26 | async-start | bytes 5013504 | tf_op jit(solution)/shard_map/while/body/eval_jaxpr/all_gather | solution.py:236
  94.5 13.6 all-to-all-start
  108.1 30.9 %all-to-all-start.1 = ((bf16[512,2,384]{0,2,1:T(8,128)(2,1)}), bf16[512,2,384]{0,2,1:T(8,128)(2,1)S(1)}, u32[]{:S(2)}, u32[]{:S(2)}) async-start(bf16[512,2,384]{0,2,1:T(8,128)(2,1)} %bitcast.497), calls=%async_computation.1 | async-start | bytes 1572864 | tf_op jit(solution)/shard_map/while/body/eval_jaxpr/all_to_all | solution.py:263
  138.9 15.6 %all-to-all-start.2 = ((bf16[512,2,384]{0,2,1:T(8,128)(2,1)}), bf16[512,2,384]{0,2,1:T(8,128)(2,1)S(1)}, u32[]{:S(2)}, u32[]{:S(2)}) async-start(bf16[512,2,384]{0,2,1:T(8,128)(2,1)} %bitcast.458), calls=%async_computation.2 | async-start | bytes 1572864 | tf_op jit(solution)/shard_map/while/body/eval_jaxpr/all_to_all | solution.py:264
  167.9 14.3 %all-to-all-start.3 = ((bf16[2,512,384]{1,2,0:T(8,128)(2,1)}), bf16[2,512,384]{1,2,0:T(8,128)(2,1)S(1)}, u32[]{:S(2)}, u32[]{:S(2)}) async-start(bf16[2,512,384]{1,2,0:T(8,128)(2,1)} %copy.129), calls=%async_computation.3 | async-start | bytes 1572864 | tf_op jit(solution)/shard_map/while/body/eval_jaxpr/all_to_all | solution.py:269
  307.2 21.4 %all-to-all-start.4 = ((bf16[512,2,384]{2,0,1:T(8,128)(2,1)}), bf16[512,2,384]{2,0,1:T(8,128)(2,1)}, u32[]{:S(2)}, u32[]{:S(2)}) async-start(bf16[512,2,384]{2,0,1:T(8,128)(2,1)} %bitcast.495), calls=%async_computation.4 | async-start | bytes 1572864 | tf_op jit(solution)/shard_map/while/body/eval_jaxpr/all_to_all | solution.py:317
  363.4 16.0 %all-to-all-start.7 = ((bf16[2,512,384]{1,2,0:T(8,128)(2,1)}), bf16[2,512,384]{1,2,0:T(8,128)(2,1)}, u32[]{:S(2)}, u32[]{:S(2)}) async-start(bf16[2,512,384]{1,2,0:T(8,128)(2,1)} %copy.133), calls=%async_computation.7 | async-start | bytes 1572864 | tf_op jit(solution)/shard_map/while/body/eval_jaxpr/all_to_all | solution.py:331
  379.4 14.2 %all-to-all-start.5 = ((bf16[2,512,384]{1,2,0:T(8,128)(2,1)}), bf16[2,512,384]{1,2,0:T(8,128)(2,1)S(1)}, u32[]{:S(2)}, u32[]{:S(2)}) async-start(bf16[2,512,384]{1,2,0:T(8,128)(2,1)} %get-tuple-element.1240), calls=%async_computation.5 | async-start | bytes 1572864 | tf_op jit(solution)/shard_map/while/body/eval_jaxpr/all_to_all | solution.py:335
  414.9 76.4 %all-gather.9.cloned.1.call-start = ((), (), s32[]{:S(2)}) async-start(), calls=%async_computation.22 | async-start | bytes 1253376 | tf_op jit(solution)/shard_map/while/body/eval_jaxpr/all_gather | solution.py:225
  415.7 89.4 %all-gather.11.cloned.1.call-start = ((), (), s32[]{:S(2)}) async-start(), calls=%async_computation.23 | async-start | bytes 1253376 | tf_op jit(solution)/shard_map/while/body/eval_jaxpr/all_gather | solution.py:227
  416.4 116.7 %all-gather.13.cloned.1.call-start = ((), (), s32[]{:S(2)}) async-start(), calls=%async_computation.24 | async-start | bytes 1253376 | tf_op jit(solution)/shard_map/while/body/eval_jaxpr/all_gather | solution.py:228
  417.2 157.7 %all-gather.15.cloned.1.call-start = ((), (), s32[]{:S(2)}) async-start(), calls=%async_computation.25 | async-start | bytes 1253376 | tf_op jit(solution)/shard_map/while/body/eval_jaxpr/all_gather | solution.py:230
  417.7 209.0 %all-gather.7.cloned.1.call-start = ((), (), s32[]{:S(2)}) async-start(), calls=%async_computation.21 | async-start | bytes 5013504 | tf_op jit(solution)/shard_map/while/body/eval_jaxpr/all_gather | solution.py:234
  418.5 262.1 %all-gather.17.cloned.1.call-start = ((), (), s32[]{:S(2)}) async-start(), calls=%async_computation.26 | async-start | bytes 5013504 | tf_op jit(solution)/shard_map/while/body/eval_jaxpr/all_gather | solution.py:236
  508.3 31.2 %all-to-all-start.1 = ((bf16[512,2,384]{0,2,1:T(8,128)(2,1)}), bf16[512,2,384]{0,2,1:T(8,128)(2,1)S(1)}, u32[]{:S(2)}, u32[]{:S(2)}) async-start(bf16[512,2,384]{0,2,1:T(8,128)(2,1)} %bitcast.497), calls=%async_computation.1 | async-start | bytes 1572864 | tf_op jit(solution)/shard_map/while/body/eval_jaxpr/all_to_all | solution.py:263
  539.5 15.2 %all-to-all-start.2 = ((bf16[512,2,384]{0,2,1:T(8,128)(2,1)}), bf16[512,2,384]{0,2,1:T(8,128)(2,1)S(1)}, u32[]{:S(2)}, u32[]{:S(2)}) async-start(bf16[512,2,384]{0,2,1:T(8,128)(2,1)} %bitcast.458), calls=%async_computation.2 | async-start | bytes 1572864 | tf_op jit(solution)/shard_map/while/body/eval_jaxpr/all_to_all | solution.py:264
  568.1 14.6 %all-to-all-start.3 = ((bf16[2,512,384]{1,2,0:T(8,128)(2,1)}), bf16[2,512,384]{1,2,0:T(8,128)(2,1)S(1)}, u32[]{:S(2)}, u32[]{:S(2)}) async-start(bf16[2,512,384]{1,2,0:T(8,128)(2,1)} %copy.129), calls=%async_computation.3 | async-start | bytes 1572864 | tf_op jit(solution)/shard_map/while/body/eval_jaxpr/all_to_all | solution.py:269
  707.8 26.7 %all-to-all-start.4 = ((bf16[512,2,384]{2,0,1:T(8,128)(2,1)}), bf16[512,2,384]{2,0,1:T(8,128)(2,1)}, u32[]{:S(2)}, u32[]{:S(2)}) async-start(bf16[512,2,384]{2,0,1:T(8,128)(2,1)} %bitcast.495), calls=%async_computation.4 | async-start | bytes 1572864 | tf_op jit(solution)/shard_map/while/body/eval_jaxpr/all_to_all | solution.py:317
  769.5 16.0 %all-to-all-start.7 = ((bf16[2,512,384]{1,2,0:T(8,128)(2,1)}), bf16[2,512,384]{1,2,0:T(8,128)(2,1)}, u32[]{:S(2)}, u32[]{:S(2)}) async-start(bf16[2,512,384]{1,2,0:T(8,128)(2,1)} %copy.133), calls=%async_computation.7 | async-start | bytes 1572864 | tf_op jit(solution)/shard_map/while/body/eval_jaxpr/all_to_all | solution.py:331
  785.5 14.1 %all-to-all-start.5 = ((bf16[2,512,384]{1,2,0:T(8,128)(2,1)}), bf16[2,512,384]{1,2,0:T(8,128)(2,1)S(1)}, u32[]{:S(2)}, u32[]{:S(2)}) async-start(bf16[2,512,384]{1,2,0:T(8,128)(2,1)} %get-tuple-element.1240), calls=%async_computation.5 | async-start | bytes 1572864 | tf_op jit(solution)/shard_map/while/body/eval_jaxpr/all_to_all | solution.py:335
  824.9 65.4 %reduce-scatter.7.cloned.1.call-start = ((), (), s32[]{:S(2)}) async-start(), calls=%async_computation.14 | async-start | bytes 2506752 | tf_op jit(solution)/shard_map/reduce_scatter | solution.py:374
  825.5 130.9 %reduce-scatter.9.cloned.1.call-start = ((), (), s32[]{:S(2)}) async-start(), calls=%async_computation.15 | async-start | bytes 2506752 | tf_op jit(solution)/shard_map/reduce_scatter | solution.py:374
  826.1 196.4 %reduce-scatter.11.cloned.1.call-start = ((), (), s32[]{:S(2)}) async-start(), calls=%async_computation.16 | async-start | bytes 2506752 | tf_op jit(solution)/shard_map/reduce_scatter | solution.py:374
  826.7 262.1 %reduce-scatter.13.cloned.1.call-start = ((), (), s32[]{:S(2)}) async-start(), calls=%async_computation.17 | async-start | bytes 2506752 | tf_op jit(solution)/shard_map/reduce_scatter | solution.py:374
  827.4 375.7 %reduce-scatter.15.cloned.1.call-start = ((), (), s32[]{:S(2)}) async-start(), calls=%async_computation.18 | async-start | bytes 10027008 | tf_op jit(solution)/shard_map/reduce_scatter | solution.py:374
  828.2 489.9 %reduce-scatter.17.cloned.1.call-start = ((), (), s32[]{:S(2)}) async-start(), calls=%async_computation.19 | async-start | bytes 10027008 | tf_op jit(solution)/shard_map/reduce_scatter | solution.py:374
  829.0 563.4 %all-reduce.35.cloned.1.call-start = ((), (), s32[]{:S(2)}) async-start(), calls=%async_computation.20 | async-start | bytes 1769472 | tf_op jit(solution)/shard_map/psum | solution.py:375
  (216 other events, 6747.3 us)
Sparse Core Ops, SparseCore 0:
  12.4 41.1 all-gather.8
  55.9 37.1 all-gather.10
  95.4 37.1 all-gather.12
  134.7 37.1 all-gather.14
  174.0 52.0 all-gather.6
  228.2 51.6 all-gather.16
  418.0 36.2 all-gather.8
  456.5 37.1 all-gather.10
  496.0 37.0 all-gather.12
  535.2 37.1 all-gather.14
  574.7 51.9 all-gather.6
  628.9 51.6 all-gather.16
Sparse Core Ops, SparseCore 1:
  829.2 61.1 reduce-scatter.6
  894.0 62.4 reduce-scatter.8
  960.1 62.3 reduce-scatter.10
  1026.3 62.4 reduce-scatter.12
  1092.9 110.2 reduce-scatter.14
  1207.2 110.8 reduce-scatter.16
  1321.7 36.0 all-reduce.34
where the time goes:
time: 1410 us
  waiting for transfers between devices  749 us (53%)
  matrix products  230 us (16%)
  blocking collectives  187 us (13%)
  other arithmetic  80.2 us (6%)
  local copies, waits for them, and re-layouts  76.8 us (5%)
  starting transfers between devices  62.2 us (4%)
  between operations  17.6 us (1%)
    reduce_scatter x6, waiting for transfers between devices, on_device(): owned = lax.psum_scatter(sums, 'fsdp', scatter_dimension=0, tiled=True)  481 us
    while x2, blocking collectives  121 us
    all_gather x2, waiting for transfers between devices, one_batch(): lax.all_gather(shards[9], 'fsdp', axis=0, tiled=True)  79.3 us
    dot_general x12, matrix products, matmul(): return jnp.dot(left, right, preferred_element_type=jnp.float32)  71.6 us
    all_gather x2, waiting for transfers between devices, one_batch(): lax.all_gather(shards[11], 'fsdp', axis=0, tiled=True)  68.3 us
    unnamed x1, blocking collectives  60.3 us
    dot_general x12, matrix products, transposed_times(): lax.dot_general(left, right, (((0,), (0,)), ((), ())), preferred_element_...  55.8 us
    all_gather x2, waiting for transfers between devices, one_batch(): lax.all_gather(shards[3], 'fsdp', axis=0, tiled=True)  42.2 us
  transfers between devices with their start and end apart: 35, of which 22 were waited for; matrix products, arithmetic and copies ran while one was open for 16% of the time, Pallas kernels for 0%

commit v1 on v0

--- a/solution.py
+++ b/solution.py
@@ -154,7 +154,7 @@
     return (slope_query, slope_keys, slope_values)
 
 
-def on_device(
+def on_device_general(
     hidden,
     segments,
     block_perm,
@@ -376,6 +376,268 @@
     return (layer_out, hidden_grad) + tuple(sums)
 
 
+def attention_forward(query, keys, values, segment_row, block_perm):
+    return attend_forward(query, keys, values, segment_row, block_perm, HD)
+
+
+def attention_backward(query, keys, values, slope, segment_row, block_perm, log_totals):
+    return attend_backward(
+        query, keys, values, slope, segment_row, block_perm, log_totals, HD
+    )
+
+
+def to_whole_sequences(array):
+    return lax.all_to_all(array, "seq", split_axis=0, concat_axis=1, tiled=True)
+
+
+def to_token_shards(array):
+    return lax.all_to_all(array, "seq", split_axis=1, concat_axis=0, tiled=True)
+
+
+def sum_over_seq(array):
+    if lax.axis_size("seq") == 2:
+        return array + lax.ppermute(array, "seq", [(0, 1), (1, 0)])
+    return lax.psum(array, "seq")
+
+
+def on_device_whole(
+    hidden,
+    segments,
+    block_perm,
+    query_weight,
+    query_bias,
+    key_weight,
+    value_weight,
+    value_bias,
+    output_weight,
+    output_bias,
+    first_gain,
+    first_shift,
+    inner_weight,
+    inner_bias,
+    outer_weight,
+    outer_bias,
+    second_gain,
+    second_shift,
+    cotangent,
+):
+    f32 = jnp.float32
+    bf16 = jnp.bfloat16
+    micro = hidden.shape[0]
+    seqs = lax.axis_size("seq")
+    owners = lax.axis_size("fsdp")
+    each = micro // seqs
+    part, width = query_weight.shape
+    wide = inner_weight.shape[1]
+    spans = wide // width
+    small = (
+        query_bias,
+        value_bias,
+        output_bias,
+        first_gain,
+        first_shift,
+        outer_bias,
+        second_gain,
+        second_shift,
+        inner_bias,
+    )
+    small_sizes = [piece.shape[0] for piece in small]
+    small_count = sum(small_sizes)
+    small_rows = -(-small_count // (16 * width)) * 16
+
+    def small_block(pieces, lead):
+        flat = jnp.concatenate(pieces, axis=-1)
+        flat = jnp.pad(flat, [(0, 0)] * len(lead) + [(0, small_rows * width - small_count)])
+        return flat.reshape(lead + (small_rows, width))
+
+    early_pack = jnp.concatenate(
+        [query_weight, key_weight, value_weight, small_block(small, ())], axis=0
+    )
+    late_pack = jnp.concatenate(
+        [output_weight]
+        + [inner_weight[:, c * width : (c + 1) * width] for c in range(spans)]
+        + [outer_weight],
+        axis=0,
+    )
+    early = lax.all_gather(early_pack, "fsdp", axis=0, tiled=False)
+    late = lax.all_gather(late_pack, "fsdp", axis=0, tiled=False)
+
+    rows_all = to_whole_sequences(hidden)
+    cot_all = to_whole_sequences(cotangent)
+    segment_rows = lax.dynamic_slice_in_dim(segments, lax.axis_index("seq") * each, each, 0)
+
+    def square(pack, index):
+        return pack[:, index * part : (index + 1) * part].reshape(width, width)
+
+    whole_query, whole_key, whole_value = (square(early, i) for i in range(3))
+    flat_small = early[:, 3 * part :].reshape(owners, small_rows * width)
+    vectors = []
+    at = 0
+    for size in small_sizes:
+        vectors.append(flat_small[:, at : at + size].reshape(owners * size).astype(f32))
+        at += size
+    (
+        query_shift,
+        value_shift,
+        output_shift,
+        gain_one,
+        shift_one,
+        outer_shift,
+        gain_two,
+        shift_two,
+        inner_shift,
+    ) = vectors
+    whole_output = square(late, 0)
+    whole_inner = jnp.concatenate([square(late, 1 + c) for c in range(spans)], axis=1)
+    whole_outer = late[:, (1 + spans) * part :].reshape(wide, width)
+
+    length = rows_all.shape[1]
+    rows = rows_all.reshape(each * length, width)
+    grad_out = cot_all.reshape(each * length, width).astype(f32)
+
+    query = (matmul(rows, whole_query) + query_shift).astype(bf16)
+    keys = matmul(rows, whole_key).astype(bf16)
+    values = (matmul(rows, whole_value) + value_shift).astype(bf16)
+    cut = lambda array, i: array[i * length : (i + 1) * length]
+    contexts, totals = [], []
+    for i in range(each):
+        piece, total = attention_forward(
+            cut(query, i), cut(keys, i), cut(values, i), segment_rows[i], block_perm
+        )
+        contexts.append(piece)
+        totals.append(total)
+    context = jnp.concatenate(contexts, axis=0) if each > 1 else contexts[0]
+    first = rows.astype(f32) + (matmul(context, whole_output) + output_shift)
+    normed = norm_core(first, gain_one) + shift_one
+    normed_low = normed.astype(bf16)
+    inner = matmul(normed_low, whole_inner) + inner_shift
+    active = exact_gelu(inner).astype(bf16)
+    second = normed + (matmul(active, whole_outer) + outer_shift)
+    result = norm_core(second, gain_two) + shift_two
+    layer_out = to_token_shards(result.astype(bf16).reshape(each, length, width))
+
+    _, second_back = jax.vjp(norm_core, second, gain_two)
+    slope_second, grad_gain_two = second_back(grad_out)
+    grad_shift_two = jnp.sum(grad_out, axis=0)
+    slope_outer = slope_second.astype(bf16)
+    grad_outer_shift = column_sum(slope_outer)
+    grad_outer = transposed_times(active, slope_outer)
+    _, gelu_back = jax.vjp(exact_gelu, inner)
+    slope_inner = gelu_back(times_transposed(slope_outer, whole_outer))[0].astype(bf16)
+    grad_inner_shift = column_sum(slope_inner)
+    grad_inner = transposed_times(normed_low, slope_inner)
+    late_grads = jnp.concatenate(
+        [grad_inner[:, c * width : (c + 1) * width].astype(bf16).reshape(owners, part, width) for c in range(spans)]
+        + [grad_outer.astype(bf16).reshape(owners, spans * part, width)],
+        axis=1,
+    )
+    late_owned = lax.psum_scatter(late_grads, "fsdp", scatter_dimension=0, tiled=False)
+    slope_normed = slope_second + times_transposed(slope_inner, whole_inner)
+    _, first_back = jax.vjp(norm_core, first, gain_one)
+    slope_first, grad_gain_one = first_back(slope_normed)
+    grad_shift_one = jnp.sum(slope_normed, axis=0)
+    slope_attn = slope_first.astype(bf16)
+    grad_output_shift = column_sum(slope_attn)
+    grad_output = transposed_times(context, slope_attn)
+    slope_context = times_transposed(slope_attn, whole_output).astype(bf16)
+    slopes = [
+        attention_backward(
+            cut(query, i),
+            cut(keys, i),
+            cut(values, i),
+            cut(slope_context, i),
+            segment_rows[i],
+            block_perm,
+            totals[i],
+        )
+        for i in range(each)
+    ]
+    slope_query, slope_keys, slope_values = (
+        jnp.concatenate(parts, axis=0) if each > 1 else parts[0] for parts in zip(*slopes)
+    )
+    slope_rows = (
+        slope_first
+        + times_transposed(slope_query, whole_query)
+        + times_transposed(slope_keys, whole_key)
+        + times_transposed(slope_values, whole_value)
+    )
+    hidden_grad = to_token_shards(slope_rows.astype(bf16).reshape(each, length, width))
+    grad_query = transposed_times(rows, slope_query)
+    grad_query_shift = column_sum(slope_query)
+    grad_key = transposed_times(rows, slope_keys)
+    grad_value = transposed_times(rows, slope_values)
+    grad_value_shift = column_sum(slope_values)
+    small_grads = (
+        grad_query_shift,
+        grad_value_shift,
+        grad_output_shift,
+        grad_gain_one,
+        grad_shift_one,
+        grad_outer_shift,
+        grad_gain_two,
+        grad_shift_two,
+        grad_inner_shift,
+    )
+    slab = lambda array: array.astype(bf16).reshape(owners, part, width)
+    early_grads = jnp.concatenate(
+        [slab(grad_query), slab(grad_key), slab(grad_value), slab(grad_output)]
+        + [
+            small_block(
+                [piece.astype(bf16).reshape(owners, -1) for piece in small_grads], (owners,)
+            )
+        ],
+        axis=1,
+    )
+    early_owned = lax.psum_scatter(early_grads, "fsdp", scatter_dimension=0, tiled=False)
+    late_owned = sum_over_seq(late_owned).astype(f32)
+    early_owned = sum_over_seq(early_owned).astype(f32)
+    own = lambda pack, index: pack[index * part : (index + 1) * part]
+    small_flat = early_owned[4 * part :].reshape(small_rows * width)
+    got = []
+    at = 0
+    for size in small_sizes:
+        got.append(small_flat[at : at + size])
+        at += size
+    (
+        own_query_shift,
+        own_value_shift,
+        own_output_shift,
+        own_gain_one,
+        own_shift_one,
+        own_outer_shift,
+        own_gain_two,
+        own_shift_two,
+        own_inner_shift,
+    ) = got
+    own_inner = jnp.concatenate([own(late_owned, c) for c in range(spans)], axis=1)
+    own_outer = late_owned[spans * part :]
+    return (
+        layer_out,
+        hidden_grad,
+        own(early_owned, 0),
+        own_query_shift,
+        own(early_owned, 1),
+        own(early_owned, 2),
+        own_value_shift,
+        own(early_owned, 3),
+        own_output_shift,
+        own_gain_one,
+        own_shift_one,
+        own_inner,
+        own_inner_shift,
+        own_outer,
+        own_outer_shift,
+        own_gain_two,
+        own_shift_two,
+    )
+
+
+def on_device(hidden, *rest):
+    if hidden.shape[0] % lax.axis_size("seq") == 0:
+        return on_device_whole(hidden, *rest)
+    return on_device_general(hidden, *rest)
+
+
 def solution(mesh):
     in_specs = (
         P("fsdp", "seq", None),

time: 1410 us -> 564 us (0.40)
  waiting for transfers between devices: 749 us -> 162 us
  blocking collectives: 187 us -> 0 us
  matrix products: 230 us -> 169 us
  starting transfers between devices: 62.2 us -> 21.9 us
  local copies, waits for them, and re-layouts: 76.8 us -> 115 us
    reduce_scatter x6 -> x2, waiting for transfers between devices: 481 us -> 82.8 us  [the longest x1 82.7 us: on_device_whole(): lax.psum_scatter(late_grads, 'fsdp', scatter_dimension=0, tiled=False)]
    all_gather x12 -> x2, waiting for transfers between devices: 190 us -> 21 us  [the longest x1 21 us: on_device_whole(): late = lax.all_gather(late_pack, 'fsdp', axis=0, tiled=False)]
    while x2 -> x0, blocking collectives: 121 us -> none
    unnamed x1 -> x0, blocking collectives: 60.3 us -> none
    unnamed x32 -> x180, local copies, waits for them, and re-layouts: 1.82 us -> 45.8 us
    all_to_all x16 -> x4, starting transfers between devices: 61.5 us -> 18.2 us  [the longest x2 9.26 us: to_token_shards(): return lax.all_to_all(array, 'seq', split_axis=1, concat_axis=0, tiled=True)]
    dot_general x12 -> x6, matrix products: 55.8 us -> 20.8 us  [transposed_times(): lax.dot_general(left, right, (((0,), (0,)), ((), ())), preferred_element_...]
    while x442 -> x0, local copies, waits for them, and re-layouts: 30.9 us -> none
  transfers between devices with their start and end apart: 35 -> 10, of which waited for: 22 -> 6; matrix products, arithmetic and copies ran while one was open for 16% -> 27% of each run, Pallas kernels for 0% -> 0%
where the time goes in v1:
time: 564 us; the launch traced here: 562 us
  matrix products  169 us (30%)
  waiting for transfers between devices  162 us (29%)
  local copies, waits for them, and re-layouts  115 us (20%)
  other arithmetic  78.8 us (14%)
  starting transfers between devices  21.9 us (4%)
  between operations  15.3 us (3%)
    reduce_scatter x1, waiting for transfers between devices, on_device_whole(): lax.psum_scatter(late_grads, 'fsdp', scatter_dimension=0, tiled=False)  82.7 us
    dot_general x6, matrix products, matmul(): return jnp.dot(left, right, preferred_element_type=jnp.float32)  68.8 us
    unnamed x180, local copies, waits for them, and re-layouts  45.8 us
    dot_general x6, matrix products, times_transposed(): lax.dot_general(left, right, (((1,), (1,)), ((), ())), preferred_element_...  35.2 us
    all_to_all x2, waiting for transfers between devices, to_whole_sequences(): return lax.all_to_all(array, 'seq', split_axis=0, concat_axis=1, tiled=True)  33.2 us
    unnamed x5, other arithmetic  22.8 us
    all_gather x1, waiting for transfers between devices, on_device_whole(): late = lax.all_gather(late_pack, 'fsdp', axis=0, tiled=False)  21 us
    dot_general x6, matrix products, transposed_times(): lax.dot_general(left, right, (((0,), (0,)), ((), ())), preferred_element_...  20.8 us
  transfers between devices with their start and end apart: 10, of which 6 were waited for; matrix products, arithmetic and copies ran while one was open for 27% of the time, Pallas kernels for 0%

profile of v1, /device:TPU:0, one launch (start us, length us, event | category | flops | bytes accessed | tf_op | source)
XLA Modules:
  0.0 562.2 jit_solution(16016713034195530011)
XLA Ops:
  7.2 6.1 %concatenate.30 = bf16[576]{0:T(1024)(128)(2,1)S(1)} concatenate(bf16[48]{0:T(256)(128)(2,1)} %param.25, bf16[48]{0:T(256)(128)(2,1)} %param.28, bf16[48]{0:T(256)(128)(2,1)} %param.30, bf16[48]{0:T(256)(128)(2,1)} %param.31, bf16[48]{0:T(256)(128)(2,1)} %param.32, bf16[48]{0:T(256)(128)(2,1)} %param.36, bf16[48]{0:T(256)(128)(2,1)} %param.37, bf16[48]{0:T(256)(128)(2,1)} %param.38, ...), dimensions={0} | concatenate | bytes 2304 | tf_op jit(solution)/shard_map/concatenate | solution.py:449
  21.5 4.2 all-to-all-start
  25.8 20.1 %all-to-all-done = bf16[2,512,768]{2,1,0:T(8,128)(2,1)S(1)} async-done(((bf16[2,512,768]{2,1,0:T(8,128)(2,1)}), bf16[2,512,768]{2,1,0:T(8,128)(2,1)S(1)}, u32[]{:S(2)}, u32[]{:S(2)}) %all-to-all-start) | async-done | bytes 1572896 | tf_op jit(solution)/shard_map/all_to_all | solution.py:390
  45.9 4.7 all-to-all-start.2
  56.5 13.0 %all-to-all-done.2 = bf16[2,512,768]{2,1,0:T(8,128)(2,1)} async-done(((bf16[2,512,768]{2,1,0:T(8,128)(2,1)}), bf16[2,512,768]{2,1,0:T(8,128)(2,1)}, u32[]{:S(2)}, u32[]{:S(2)}) %all-to-all-start.2) | async-done | bytes 1572896 | tf_op jit(solution)/shard_map/all_to_all | solution.py:390
  76.3 3.9 fusion.77
  85.6 3.5 fusion.22
  113.0 7.2 %fusion.84 = (f32[12,512]{1,0:T(8,128)S(1)}, f32[12,512,512]{1,2,0:T(8,128)}) fusion(bf16[512,12,64]{0,2,1:T(8,128)(2,1)S(1)} %bitcast.333, bf16[12,512,64]{1,2,0:T(8,128)(2,1)S(1)} %copy-done.13, pred[12]{0:T(512)(128)(4,1)S(1)} %copy-done.65, s32[12,512]{1,0:T(8,128)S(1)} %copy-done.55, s32[512]{0:T(512)S(1)} %bitcast.339), kind=kOutput, calls=%fused_computation.204 | convolution fusion | flops 421914624 | bytes 14206988 | tf_op jit(solution)/shard_map/qhd,hkd->hqk/dot_general | solution.py:54
  120.2 6.4 %fusion.9 = f32[12,512]{1,0:T(8,128)S(1)} fusion(f32[12,512,512]{1,2,0:T(8,128)} %get-tuple-element.126, f32[12,512]{1,0:T(8,128)S(1)} %get-tuple-element.125), kind=kLoop, calls=%fused_computation.39 | loop fusion | flops 6285312 | bytes 12632064 | tf_op jit(solution)/shard_map/reduce_sum | solution.py:94
  135.2 21.0 %all-gather.7.cloned.1.call-done = bf16[6912,768]{1,0:T(8,128)(2,1)} async-done(((bf16[432,768]{1,0:T(8,128)(2,1)}), bf16[6912,768]{1,0:T(8,128)(2,1)}) %all-gather.7.cloned.1.call-update) | async-done | bytes 10616848 | tf_op jit(solution)/shard_map/all_gather | solution.py:463
  159.0 6.3 %fusion.75 = (bf16[16,48,768]{2,1,0:T(8,128)(2,1)S(1)}, bf16[16,48,768]{2,1,0:T(8,128)(2,1)S(1)}, bf16[16,48,768]{2,1,0:T(8,128)(2,1)}, bf16[16,48,768]{2,1,0:T(8,128)(2,1)}, bf16[16,48,768]{2,1,0:T(8,128)(2,1)S(1)}) fusion(bf16[16,432,768]{2,1,0:T(8,128)(2,1)} %bitcast.275), kind=kLoop, calls=%fused_computation.195 | loop fusion | bytes 11796480 | tf_op jit(solution)/shard_map/slice | solution.py:470
  169.8 51.1 %multiply_convert_fusion.2 = (bf16[1024,3072]{1,0:T(8,128)(2,1)}, f32[1024,3072]{1,0:T(8,128)}, f32[1024,3072]{1,0:T(8,128)}) fusion(f32[3072]{0:T(1024)S(1)} %reshape.508, bf16[768,768]{1,0:T(8,128)(2,1)S(1)} %bitcast.317, bf16[768,768]{1,0:T(8,128)(2,1)S(1)} %bitcast.320, bf16[768,768]{1,0:T(8,128)(2,1)S(1)} %bitcast.322, ...), kind=kOutput, calls=%fused_computation.15 | convolution fusion | flops 5062262784 | bytes 39348224 | tf_op jit(solution)/shard_map/dot_general | solution.py:29
  220.9 7.7 %fusion.87 = (f32[1024]{0:T(1024)S(1)}, f32[1024,768]{0,1:T(8,128)S(1)}) fusion(f32[768]{0:T(1024)S(1)} %copy-done.67, bf16[1024,3072]{1,0:T(8,128)(2,1)} %get-tuple-element.67, bf16[3072,768]{1,0:T(8,128)(2,1)S(1)} %bitcast.297, f32[768]{0:T(1024)S(1)} %reshape.507, f32[768]{0:T(1024)S(1)} %reshape.506, f32[1024]{0:T(1024)S(1)} %fusion.49, ...), kind=kOutput, calls=%fused_computation.207 | convolution fusion | flops 4837342208 | bytes 17323008 | tf_op jit(solution)/shard_map/dot_general | solution.py:29
  235.5 18.4 %fusion.90 = (bf16[3072]{0:T(1024)(128)(2,1)S(1)}, bf16[1024,3072]{1,0:T(8,128)(2,1)}) fusion(f32[1024,3072]{1,0:T(8,128)} %get-tuple-element.68, bf16[1024,768]{0,1:T(8,128)(2,1)} %get-tuple-element.58, bf16[3072,768]{1,0:T(8,128)(2,1)} %bitcast.298, f32[1024,3072]{1,0:T(8,128)} %get-tuple-element.131, f32[3072]{0:T(1024)S(1)} %reshape.508), kind=kOutput, calls=%fused_computation.210 | convolution fusion | flops 4882166784 | bytes 37767168 | tf_op jit(solution)/shard_map/dot_general | solution.py:33
  253.9 10.0 %multiply_reduce_fusion.3 = (bf16[768]{0:T(1024)(128)(2,1)S(1)}, f32[1024]{0:T(1024)S(1)}, bf16[768]{0:T(1024)(128)(2,1)S(1)}, f32[1024,768]{0,1:T(8,128)S(1)}) fusion(f32[1024,768]{0,1:T(8,128)S(1)} %get-tuple-element.130, f32[1024]{0:T(1024)S(1)} %fusion.49, f32[1024]{0:T(1024)S(1)} %broadcast_multiply_fusion.1, f32[768]{0:T(1024)S(1)} %reshape.506, ...), kind=kOutput, calls=%fused_computation.54 | convolution fusion | flops 4858573824 | bytes 20469760 | tf_op jit(solution)/shard_map/dot_general | solution.py:33
  273.2 4.2 fusion.29
  277.4 7.2 %multiply_reduce_fusion = (f32[12,512]{1,0:T(8,128)S(1)}, f32[12,512,512]{1,2,0:T(8,128)}) fusion(f32[12,512,512]{1,2,0:T(8,128)S(1)} %bitcast.265, f32[12,512]{1,0:T(8,128)S(1)} %copy-done.50, bf16[512,12,64]{0,2,1:T(8,128)(2,1)} %bitcast.279, bf16[12,512,64]{1,2,0:T(8,128)(2,1)S(1)} %copy-done.10, pred[12]{0:T(512)(128)(4,1)S(1)} %copy-done.66), kind=kOutput, calls=%fused_computation.9 | convolution fusion | flops 412477440 | bytes 26787852 | tf_op jit(solution)/shard_map/qhd,hkd->hqk/dot_general | solution.py:124
  284.6 10.8 %multiply_convert_fusion = bf16[12,512,512]{1,2,0:T(8,128)(2,1)S(1)} fusion(f32[12,512,512]{1,2,0:T(8,128)} %get-tuple-element.138, f32[12,512,512]{1,2,0:T(8,128)} %get-tuple-element.126, f32[12,512]{1,0:T(8,128)S(1)} %get-tuple-element.137, f32[12,512]{1,0:T(8,128)S(1)} %copy-done.50), kind=kLoop, calls=%fused_computation.8 | loop fusion | flops 12582912 | bytes 31506432 | tf_op jit(solution)/shard_map/convert_element_type | solution.py:128
  303.5 5.9 %multiply_reduce_fusion.1 = (f32[12,512]{1,0:T(8,128)S(1)}, f32[12,512,512]{1,2,0:T(8,128)}) fusion(f32[12,512,512]{1,2,0:T(8,128)S(1)} %bitcast.263, f32[12,512]{1,0:T(8,128)S(1)} %copy-done.49, bf16[512,12,64]{0,2,1:T(8,128)(2,1)S(1)} %bitcast.277, bf16[12,512,64]{1,2,0:T(8,128)(2,1)S(1)} %copy-done.8, pred[12]{0:T(512)(128)(4,1)S(1)} %copy-done.64), kind=kOutput, calls=%fused_computation.12 | convolution fusion | flops 412477440 | bytes 26787852 | tf_op jit(solution)/shard_map/qhd,hkd->hqk/dot_general | solution.py:124
  309.4 6.9 %multiply_convert_fusion.1 = bf16[12,512,512]{1,2,0:T(8,128)(2,1)S(1)} fusion(f32[12,512,512]{1,2,0:T(8,128)} %get-tuple-element.136, f32[12,512,512]{1,2,0:T(8,128)S(1)} %bitcast.263, f32[12,512]{1,0:T(8,128)S(1)} %get-tuple-element.135, f32[12,512]{1,0:T(8,128)S(1)} %copy-done.49), kind=kLoop, calls=%fused_computation.11 | loop fusion | flops 12582912 | bytes 31506432 | tf_op jit(solution)/shard_map/convert_element_type | solution.py:128
  321.3 11.3 %fusion.71 = (bf16[12,64]{1,0:T(8,128)(2,1)S(1)}, bf16[2,512,12,64]{1,0,3,2:T(2,128)(2,1)}, bf16[2,512,12,64]{1,0,3,2:T(2,128)(2,1)}) fusion(bf16[512,12,64]{0,2,1:T(8,128)(2,1)S(1)} %copy-done.25, pred[2,12]{0,1:T(8,128)(4,1)S(1)} %copy-done.60, bf16[512,12,64]{0,2,1:T(8,128)(2,1)S(1)} %copy-done.24, pred[2,12]{0,1:T(8,128)(4,1)S(1)} %copy-done.61, ...), kind=kLoop, calls=%fused_computation.192 | loop fusion | flops 3931392 | bytes 6293040 | tf_op jit(solution)/shard_map/reduce_sum | solution.py:45
  348.2 8.5 %convolution_convert_fusion.1 = bf16[768,3072]{1,0:T(8,128)(2,1)S(1)} fusion(bf16[1024,3072]{1,0:T(8,128)(2,1)} %get-tuple-element.144, f32[1024,768]{0,1:T(8,128)S(1)} %copy-done.6, f32[768]{0:T(1024)S(1)} %reshape.507, f32[768]{0:T(1024)S(1)} %reshape.506, f32[1024]{0:T(1024)S(1)} %fusion.49, f32[1024]{0:T(1024)S(1)} %broadcast_multiply_fusion.1), kind=kOutput, calls=%fused_computation.49 | convolution fusion | flops 4838129664 | bytes 14170112 | tf_op jit(solution)/shard_map/dot_general | solution.py:39
  362.3 5.5 convolution_convert_fusion
  370.4 7.4 %copy.97 = bf16[1,1024,768]{2,0,1:T(2,128)(2,1)S(1)} copy(bf16[1,1024,768]{1,2,0:T(8,128)(2,1)} %get-tuple-element.81) | data formatting | bytes 3145728 | tf_op jit(solution)/shard_map/reshape | solution.py:517
  378.4 11.4 %reduce.16 = bf16[1024,768]{1,0:T(8,128)(2,1)} reduce(bf16[1024,1,768]{2,1,0:T(2,128)(2,1)S(1)} %bitcast.270, bf16[]{:T(256)} %broadcast.625), dimensions={1}, to_apply=%bitcast.188.reduce_sub_computation | reduce | bytes 3145730
  392.4 4.6 all-to-all-start.1
  404.2 7.5 %copy.109 = bf16[1,1024,768]{2,0,1:T(2,128)(2,1)S(1)} copy(bf16[1,1024,768]{1,2,0:T(8,128)(2,1)} %fusion.25) | data formatting | bytes 3145728 | tf_op jit(solution)/shard_map/reshape | solution.py:564
  411.6 11.4 %reduce.17 = bf16[1024,768]{1,0:T(8,128)(2,1)} reduce(bf16[1024,1,768]{2,1,0:T(2,128)(2,1)S(1)} %bitcast.271, bf16[]{:T(256)} %broadcast.625), dimensions={1}, to_apply=%bitcast.190.reduce_sub_computation | reduce | bytes 3145730
  425.5 4.6 all-to-all-start.3
  436.5 14.4 %all-to-all-done.3 = bf16[2,2,196608]{2,1,0:T(2,128)(2,1)} async-done(((bf16[2,2,196608]{2,1,0:T(2,128)(2,1)}), bf16[2,2,196608]{2,1,0:T(2,128)(2,1)}, u32[]{:S(2)}, u32[]{:S(2)}) %all-to-all-start.3) | async-done | bytes 1572896 | tf_op jit(solution)/shard_map/all_to_all | solution.py:394
  454.8 82.7 %reduce-scatter.5.cloned.1.call-done = bf16[1,384,768]{2,1,0:T(8,128)(2,1)} async-done(((bf16[16,384,768]{2,1,0:T(8,128)(2,1)}), bf16[1,384,768]{2,1,0:T(8,128)(2,1)}) %reduce-scatter.5.cloned.1.call-update) | async-done | bytes 589840 | tf_op jit(solution)/shard_map/reduce_scatter | solution.py:534
  542.0 10.5 %collective-permute-done.1 = bf16[384,768]{1,0:T(8,128)(2,1)S(1)} collective-permute-done((bf16[384,768]{1,0:T(8,128)(2,1)}, bf16[384,768]{1,0:T(8,128)(2,1)S(1)}, u32[]{:S(2)}, u32[]{:S(2)}) %collective-permute-start.1) | collective-permute-done | bytes 589856 | tf_op jit(solution)/shard_map/ppermute | solution.py:399
  (304 shorter events, 148.4 us)
Async XLA Ops:
  7.2 18.5 %copy-start.59 = (s32[12,2]{0,1:T(2,128)S(1)}, s32[12,2]{0,1:T(2,128)}, u32[]{:S(2)}) copy-start(s32[12,2]{0,1:T(2,128)} %param.23) | copy-start | bytes 292
  7.2 67.2 %all-gather.5.cloned.1.call-start = ((), (), s32[]{:S(2)}) async-start(), calls=%async_computation.8 | async-start | bytes 4177920 | tf_op jit(solution)/shard_map/all_gather | solution.py:462
  15.1 141.2 %all-gather.7.cloned.1.call-start = ((), (), s32[]{:S(2)}) async-start(), calls=%async_computation.9 | async-start | bytes 11280384 | tf_op jit(solution)/shard_map/all_gather | solution.py:463
  21.5 29.2 %copy-start.62 = (s32[2,1024]{1,0:T(2,128)S(1)}, s32[2,1024]{1,0:T(2,128)}, u32[]{:S(2)}) copy-start(s32[2,1024]{1,0:T(2,128)} %param.22) | copy-start | bytes 24580
  21.5 24.4 %all-to-all-start = ((bf16[2,512,768]{2,1,0:T(8,128)(2,1)}), bf16[2,512,768]{2,1,0:T(8,128)(2,1)S(1)}, u32[]{:S(2)}, u32[]{:S(2)}) async-start(bf16[2,512,768]{2,1,0:T(8,128)(2,1)} %param.21), calls=%async_computation | async-start | bytes 3145728 | tf_op jit(solution)/shard_map/all_to_all | solution.py:390
  45.9 10.6 %copy-start.15 = (bf16[2,512,768]{2,1,0:T(8,128)(2,1)}, bf16[2,512,768]{2,1,0:T(8,128)(2,1)S(1)}, u32[]{:S(2)}) copy-start(bf16[2,512,768]{2,1,0:T(8,128)(2,1)S(1)} %all-to-all-done) | copy-start | bytes 4718596
  45.9 23.7 %all-to-all-start.2 = ((bf16[2,512,768]{2,1,0:T(8,128)(2,1)}), bf16[2,512,768]{2,1,0:T(8,128)(2,1)}, u32[]{:S(2)}, u32[]{:S(2)}) async-start(bf16[2,512,768]{2,1,0:T(8,128)(2,1)} %param.39), calls=%async_computation.2 | async-start | bytes 3145728 | tf_op jit(solution)/shard_map/all_to_all | solution.py:390
  50.6 379.6 %reduce-scatter.3.cloned.1.call-start = ((), (), s32[]{:S(2)}) async-start(), calls=%async_computation.6 | async-start | bytes 5431296 | tf_op jit(solution)/shard_map/reduce_scatter | solution.py:591
  85.0 44.2 %copy-start.9 = (bf16[12,512,64]{1,2,0:T(8,128)(2,1)}, bf16[12,512,64]{1,2,0:T(8,128)(2,1)S(1)}, u32[]{:S(2)}) copy-start(bf16[12,512,64]{1,2,0:T(8,128)(2,1)S(1)} %gather_fusion.4) | copy-start | bytes 2359300
  85.6 41.0 %copy-start.7 = (bf16[12,512,64]{1,2,0:T(8,128)(2,1)}, bf16[12,512,64]{1,2,0:T(8,128)(2,1)S(1)}, u32[]{:S(2)}) copy-start(bf16[12,512,64]{1,2,0:T(8,128)(2,1)S(1)} %gather_fusion.2) | copy-start | bytes 2359300
  106.6 6.3 %copy-start.47 = (bf16[512,768]{0,1:T(8,128)(2,1)}, bf16[512,768]{0,1:T(8,128)(2,1)S(1)}, u32[]{:S(2)}) copy-start(bf16[512,768]{0,1:T(8,128)(2,1)S(1)} %get-tuple-element.87) | copy-start | bytes 2359300
  111.0 15.6 %copy-start = (f32[12,512,512]{1,2,0:T(8,128)}, f32[12,512,512]{1,2,0:T(8,128)S(1)}, u32[]{:S(2)}) copy-start(f32[12,512,512]{1,2,0:T(8,128)S(1)} %get-tuple-element.128) | copy-start | bytes 37748740
  133.9 31.3 %copy-start.28 = (bf16[1024,12,64]{0,2,1:T(8,128)(2,1)}, bf16[1024,12,64]{0,2,1:T(8,128)(2,1)S(1)}, u32[]{:S(2)}) copy-start(bf16[1024,12,64]{0,2,1:T(8,128)(2,1)S(1)} %pad_maximum_fusion.1) | copy-start | bytes 4718596
  158.9 62.0 %copy-start.23 = (bf16[16,192,768]{2,1,0:T(8,128)(2,1)}, bf16[16,192,768]{2,1,0:T(8,128)(2,1)S(1)}, u32[]{:S(2)}) copy-start(bf16[16,192,768]{2,1,0:T(8,128)(2,1)S(1)} %slice.279) | copy-start | bytes 14155780
  159.0 6.3 %copy-start.27 = (bf16[1024,768]{0,1:T(8,128)(2,1)S(1)}, bf16[1024,768]{0,1:T(8,128)(2,1)}, u32[]{:S(2)}) copy-start(bf16[1024,768]{0,1:T(8,128)(2,1)} %copy.122) | copy-start | bytes 4718596
  167.0 97.0 %copy-start.5 = (f32[1024,768]{0,1:T(8,128)}, f32[1024,768]{0,1:T(8,128)S(1)}, u32[]{:S(2)}) copy-start(f32[1024,768]{0,1:T(8,128)S(1)} %get-tuple-element.130) | copy-start | bytes 9437188
  167.4 53.5 %copy-start.52 = (f32[1024]{0:T(1024)}, f32[1024]{0:T(1024)S(1)}, u32[]{:S(2)}) copy-start(f32[1024]{0:T(1024)S(1)} %multiply_reduce_fusion.7) | copy-start | bytes 12292
  169.8 51.2 %copy-start.67 = (f32[768]{0:T(1024)S(1)}, f32[768]{0:T(1024)}, u32[]{:S(2)}) copy-start(f32[768]{0:T(1024)} %reshape.509) | copy-start | bytes 9220
  253.9 10.0 %copy-start.53 = (f32[1024]{0:T(1024)S(1)}, f32[1024]{0:T(1024)}, u32[]{:S(2)}) copy-start(f32[1024]{0:T(1024)} %copy-done.52) | copy-start | bytes 12292
  284.6 10.8 %copy-start.48 = (bf16[512,768]{0,1:T(8,128)(2,1)S(1)}, bf16[512,768]{0,1:T(8,128)(2,1)}, u32[]{:S(2)}) copy-start(bf16[512,768]{0,1:T(8,128)(2,1)} %copy-done.47) | copy-start | bytes 2359300
  284.6 15.9 %slice-start = ((s8[12582912]{0:T(1024)(128)(4,1)}), s8[4194304]{0:T(1024)(128)(4,1)S(1)}, s32[]{:S(2)}) async-start(s8[12582912]{0:T(1024)(128)(4,1)} %bitcast.262), calls=%async_computation.10 | async-start | bytes 8388608
  284.6 15.9 %slice-start.1 = ((s8[12582912]{0:T(1024)(128)(4,1)}), s8[4194304]{0:T(1024)(128)(4,1)S(1)}, s32[]{:S(2)}) async-start(s8[12582912]{0:T(1024)(128)(4,1)} %bitcast.262), calls=%async_computation.11 | async-start | bytes 8388608
  295.4 5.1 slice-start.2
  309.4 6.9 %copy-start.46 = (bf16[512,768]{0,1:T(8,128)(2,1)S(1)}, bf16[512,768]{0,1:T(8,128)(2,1)}, u32[]{:S(2)}) copy-start(bf16[512,768]{0,1:T(8,128)(2,1)} %copy-done.45) | copy-start | bytes 2359300
  347.0 190.5 %reduce-scatter.5.cloned.1.call-start = ((), (), s32[]{:S(2)}) async-start(), calls=%async_computation.7 | async-start | bytes 10027008 | tf_op jit(solution)/shard_map/reduce_scatter | solution.py:534
  389.8 7.3 %copy-start.31 = (bf16[1024,12,64]{0,2,1:T(8,128)(2,1)S(1)}, bf16[1024,12,64]{0,2,1:T(8,128)(2,1)}, u32[]{:S(2)}) copy-start(bf16[1024,12,64]{0,2,1:T(8,128)(2,1)} %copy-done.30) | copy-start | bytes 4718596
  389.8 7.3 %copy-start.41 = (bf16[16,48,768]{2,1,0:T(8,128)(2,1)S(1)}, bf16[16,48,768]{2,1,0:T(8,128)(2,1)}, u32[]{:S(2)}) copy-start(bf16[16,48,768]{2,1,0:T(8,128)(2,1)} %get-tuple-element.80) | copy-start | bytes 3538948
  392.4 33.2 %all-to-all-start.1 = ((bf16[2,2,196608]{2,1,0:T(2,128)(2,1)}), bf16[2,2,196608]{2,1,0:T(2,128)(2,1)}, u32[]{:S(2)}, u32[]{:S(2)}) async-start(bf16[2,2,196608]{2,1,0:T(2,128)(2,1)} %reshape.594), calls=%async_computation.1 | async-start | bytes 3145728 | tf_op jit(solution)/shard_map/all_to_all | solution.py:394
  425.5 25.3 %all-to-all-start.3 = ((bf16[2,2,196608]{2,1,0:T(2,128)(2,1)}), bf16[2,2,196608]{2,1,0:T(2,128)(2,1)}, u32[]{:S(2)}, u32[]{:S(2)}) async-start(bf16[2,2,196608]{2,1,0:T(2,128)(2,1)} %reshape.596), calls=%async_computation.3 | async-start | bytes 3145728 | tf_op jit(solution)/shard_map/all_to_all | solution.py:394
  430.2 108.8 %collective-permute-start = (bf16[208,768]{1,0:T(8,128)(2,1)}, bf16[208,768]{1,0:T(8,128)(2,1)}, u32[]{:S(2)}, u32[]{:S(2)}) collective-permute-start(bf16[208,768]{1,0:T(8,128)(2,1)} %bitcast.338), channel_id=1, source_target_pairs={{0,1},{1,0},{2,3},{3,2},{4,5},{5,4},{6,7},{7,6},{8,9},{9,8},{10,11... | collective-permute-start | bytes 958472 | tf_op jit(solution)/shard_map/ppermute | solution.py:399
  453.4 85.6 %copy-start.51 = (bf16[1,208,768]{2,1,0:T(8,128)(2,1)S(1)}, bf16[1,208,768]{2,1,0:T(8,128)(2,1)}, u32[]{:S(2)}) copy-start(bf16[1,208,768]{2,1,0:T(8,128)(2,1)} %reduce-scatter.3.cloned.1.call-done) | copy-start | bytes 958468
  537.5 15.0 %collective-permute-start.1 = (bf16[384,768]{1,0:T(8,128)(2,1)}, bf16[384,768]{1,0:T(8,128)(2,1)S(1)}, u32[]{:S(2)}, u32[]{:S(2)}) collective-permute-start(bf16[384,768]{1,0:T(8,128)(2,1)} %bitcast.335), channel_id=1, source_target_pairs={{0,1},{1,0},{2,3},{3,2},{4,5},{5,4},{6,7},{7,6},{8,9},{9,8},{10,11... | collective-permute-start | bytes 1769480 | tf_op jit(solution)/shard_map/ppermute | solution.py:399
  (56 other events, 149.9 us)
Sparse Core Ops, SparseCore 0:
  15.2 51.7 all-gather.4
  69.3 86.9 all-gather.6
  347.2 75.9 reduce-scatter.2
  427.1 110.3 reduce-scatter.4

commit v2 on v1

--- a/solution.py
+++ b/solution.py
@@ -1,6 +1,10 @@
+import functools
+
 import jax
 import jax.numpy as jnp
 from jax import lax
+from jax.experimental import pallas as pl
+from jax.experimental.pallas import tpu as pltpu
 from jax.sharding import PartitionSpec as P
 
 H = 12
@@ -376,14 +380,391 @@
     return (layer_out, hidden_grad) + tuple(sums)
 
 
-def attention_forward(query, keys, values, segment_row, block_perm):
-    return attend_forward(query, keys, values, segment_row, block_perm, HD)
-
-
-def attention_backward(query, keys, values, slope, segment_row, block_perm, log_totals):
-    return attend_backward(
-        query, keys, values, slope, segment_row, block_perm, log_totals, HD
-    )
+def dot(left, right, contract):
+    return lax.dot_general(
+        left, right, ((contract[:1], contract[1:]), ((), ())), preferred_element_type=jnp.float32
+    )
+
+
+def project_kernel(rows_ref, early_ref, small_ref, query_ref, keys_ref, values_ref):
+    rows = rows_ref[...]
+    part = part_of(early_ref)
+    width = rows.shape[1]
+    for index, (out_ref, bias) in enumerate(((query_ref, 0), (keys_ref, None), (values_ref, 1))):
+        weight = early_ref[:, index * part : (index + 1) * part, :].reshape(width, width)
+        product = dot(rows, weight, (1, 0))
+        if bias is not None:
+            product = product + small_ref[bias : bias + 1, :]
+        out_ref[...] = product.astype(jnp.bfloat16)
+
+
+def part_of(early_ref):
+    return early_ref.shape[2] // early_ref.shape[0]
+
+
+def project(rows, early, small):
+    count, width = rows.shape
+    tile = count // 2
+    token = pl.BlockSpec((tile, width), lambda i: (i, 0))
+    shape = jax.ShapeDtypeStruct((count, width), jnp.bfloat16)
+    return pl.pallas_call(
+        project_kernel,
+        grid=(2,),
+        in_specs=[
+            token,
+            pl.BlockSpec(early.shape, lambda i: (0, 0, 0), pipeline_mode=pl.Buffered(1)),
+            pl.BlockSpec(small.shape, lambda i: (0, 0)),
+        ],
+        out_specs=[token, token, token],
+        out_shape=[shape, shape, shape],
+        name="project",
+    )(rows, early, small)
+
+
+def masked_probs(query, keys, same):
+    scores = jnp.where(same, dot(keys, query, (1, 1)), -1e30)
+    lifted = jnp.exp(scores - jnp.max(scores, axis=0, keepdims=True))
+    return lifted * (1.0 / jnp.sum(lifted, axis=0, keepdims=True))
+
+
+def visible(segment_row_ref, segment_column_ref, block, target, size):
+    own = segment_row_ref[block : block + 1, :]
+    other = segment_column_ref[pl.ds(pl.multiple_of(target * size, size), size), :]
+    mirror = lax.broadcasted_iota(jnp.int32, (size, size), 0) == lax.broadcasted_iota(
+        jnp.int32, (size, size), 1
+    )
+    return (own == other) | mirror
+
+
+def attend_kernel(
+    perm_ref, query_ref, keys_ref, values_ref, segment_row_ref, segment_column_ref, out_ref
+):
+    blocks, size = segment_row_ref.shape
+    pair = query_ref.shape[1] // HD
+    scale = HD**-0.5
+    for j in range(pair):
+        lanes = slice(j * HD, (j + 1) * HD)
+        for block in range(blocks):
+            target = perm_ref[pl.program_id(0) * pair + j, block]
+            there = pl.ds(pl.multiple_of(target * size, size), size)
+            here = slice(block * size, (block + 1) * size)
+            same = visible(segment_row_ref, segment_column_ref, block, target, size)
+            query = query_ref[here, lanes] * jnp.bfloat16(scale)
+            probs = masked_probs(query, keys_ref[there, lanes], same).astype(jnp.bfloat16)
+            piece = dot(values_ref[there, lanes], probs, (0, 0))
+            out_ref[here, lanes] = piece.T.astype(jnp.bfloat16)
+
+
+def attend_back_kernel(
+    perm_ref,
+    query_ref,
+    keys_ref,
+    values_ref,
+    slope_ref,
+    segment_row_ref,
+    segment_column_ref,
+    slope_query_ref,
+    slope_keys_ref,
+    slope_values_ref,
+):
+    blocks, size = segment_row_ref.shape
+    pair = query_ref.shape[1] // HD
+    scale = HD**-0.5
+    bf16 = jnp.bfloat16
+    for j in range(pair):
+        lanes = slice(j * HD, (j + 1) * HD)
+        for block in range(blocks):
+            target = perm_ref[pl.program_id(0) * pair + j, block]
+            there = pl.ds(pl.multiple_of(target * size, size), size)
+            here = slice(block * size, (block + 1) * size)
+            same = visible(segment_row_ref, segment_column_ref, block, target, size)
+            query = query_ref[here, lanes] * bf16(scale)
+            keys = keys_ref[there, lanes]
+            slope = slope_ref[here, lanes]
+            probs = masked_probs(query, keys, same)
+            slope_probs = dot(values_ref[there, lanes], slope, (1, 1))
+            row_dot = jnp.sum(probs * slope_probs, axis=0, keepdims=True)
+            slope_scores = (probs * (slope_probs - row_dot)).astype(bf16)
+            slope_query_ref[here, lanes] = (dot(keys, slope_scores, (0, 0)) * scale).T.astype(bf16)
+            slope_keys_ref[there, lanes] = dot(slope_scores, query, (1, 0)).astype(bf16)
+            slope_values_ref[there, lanes] = dot(probs.astype(bf16), slope, (1, 0)).astype(bf16)
+
+
+def attend_call(kernel, arrays, segment_row, block_perm, outs, name):
+    count, width = arrays[0].shape
+    blocks = block_perm.shape[1]
+    lanes = 2 * HD
+    head = pl.BlockSpec((count, lanes), lambda i, perm: (0, i))
+    row = segment_row.reshape(blocks, count // blocks)
+    column = segment_row.reshape(count, 1)
+    shape = jax.ShapeDtypeStruct((count, width), jnp.bfloat16)
+    return pl.pallas_call(
+        kernel,
+        grid_spec=pltpu.PrefetchScalarGridSpec(
+            num_scalar_prefetch=1,
+            grid=(width // lanes,),
+            in_specs=[head] * len(arrays)
+            + [
+                pl.BlockSpec(row.shape, lambda i, perm: (0, 0)),
+                pl.BlockSpec(column.shape, lambda i, perm: (0, 0)),
+            ],
+            out_specs=[head] * outs,
+        ),
+        out_shape=[shape] * outs,
+        name=name,
+    )(block_perm, *arrays, row, column)
+
+
+def normalize(values):
+    average = jnp.mean(values, axis=-1, keepdims=True)
+    centered = values - average
+    spread = jnp.mean(centered * centered, axis=-1, keepdims=True)
+    factor = lax.rsqrt(spread + EPSILON)
+    return centered * factor, factor
+
+
+def normalize_back(slope, unit, factor):
+    return (
+        slope
+        - jnp.mean(slope, axis=-1, keepdims=True)
+        - unit * jnp.mean(slope * unit, axis=-1, keepdims=True)
+    ) * factor
+
+
+def middle_kernel(
+    tiles,
+    halves,
+    rows_ref,
+    context_ref,
+    cotangent_ref,
+    late_ref,
+    small_ref,
+    inner_shift_ref,
+    result_ref,
+    slope_first_ref,
+    slope_context_ref,
+    grads_ref,
+    small_grads_ref,
+    inner_shift_grad_ref,
+    active_ref,
+    slope_inner_ref,
+    slope_outer_ref,
+    normed_ref,
+    slope_attn_ref,
+    context_all_ref,
+    bend_ref,
+):
+    f32, bf16 = jnp.float32, jnp.bfloat16
+    step = pl.program_id(0)
+    owners, packed, width = late_ref.shape
+    part = width // owners
+    wide = active_ref.shape[1]
+    spans = wide // width
+    tile = rows_ref.shape[0]
+
+    def inner_weight(c):
+        return late_ref[:, (1 + c) * part : (2 + c) * part, :].reshape(width, width)
+
+    def output_weight():
+        return late_ref[:, :part, :].reshape(width, width)
+
+    def outer_weight(c):
+        few = owners // spans
+        return late_ref[c * few : (c + 1) * few, (1 + spans) * part :, :].reshape(width, width)
+
+    def total(values):
+        return jnp.sum(values, axis=0, keepdims=True)
+
+    @pl.when(step == 0)
+    def _():
+        small_grads_ref[...] = jnp.zeros_like(small_grads_ref)
+        inner_shift_grad_ref[...] = jnp.zeros_like(inner_shift_grad_ref)
+
+    @pl.when(step < tiles)
+    def _():
+        at = pl.ds(pl.multiple_of(step * tile, tile), tile)
+        vector = lambda i: small_ref[i : i + 1, :]
+        output_shift, gain_one, shift_one = vector(2), vector(3), vector(4)
+        outer_shift, gain_two, shift_two = vector(5), vector(6), vector(7)
+        context = context_ref[...]
+        context_all_ref[at, :] = context
+        attn = dot(context, output_weight(), (1, 0)) + output_shift
+        unit_one, factor_one = normalize(rows_ref[...].astype(f32) + attn)
+        normed = unit_one * gain_one + shift_one
+        normed_low = normed.astype(bf16)
+        normed_ref[at, :] = normed_low
+        outer = jnp.zeros((tile, width), f32)
+        for c in range(spans):
+            span = slice(c * width, (c + 1) * width)
+            inner = dot(normed_low, inner_weight(c), (1, 0)) + inner_shift_ref[:, span]
+            phi = 0.5 * (1.0 + lax.erf(inner * (0.5**0.5)))
+            density = jnp.exp(inner * inner * -0.5) * ((2.0 * jnp.pi) ** -0.5)
+            bend_ref[:, span] = phi + inner * density
+            active = (inner * phi).astype(bf16)
+            active_ref[at, span] = active
+            outer = outer + dot(active, outer_weight(c), (1, 0))
+        second = normed + (outer + outer_shift)
+        unit_two, factor_two = normalize(second)
+        result_ref[...] = (unit_two * gain_two + shift_two).astype(bf16)
+        cotangent = cotangent_ref[...].astype(f32)
+        slope_second = normalize_back(cotangent * gain_two, unit_two, factor_two)
+        slope_outer = slope_second.astype(bf16)
+        slope_outer_ref[at, :] = slope_outer
+        slope_normed = slope_second
+        for c in range(spans):
+            span = slice(c * width, (c + 1) * width)
+            back = dot(slope_outer, outer_weight(c), (1, 1)) * bend_ref[:, span]
+            slope_inner = back.astype(bf16)
+            slope_inner_ref[at, span] = slope_inner
+            inner_shift_grad_ref[:, span] += total(slope_inner.astype(f32))
+            slope_normed = slope_normed + dot(slope_inner, inner_weight(c), (1, 1))
+        slope_first = normalize_back(slope_normed * gain_one, unit_one, factor_one)
+        slope_first_ref[...] = slope_first
+        slope_attn = slope_first.astype(bf16)
+        slope_attn_ref[at, :] = slope_attn
+        slope_context_ref[...] = dot(slope_attn, output_weight(), (1, 1)).astype(bf16)
+        small_grads_ref[2:3, :] += total(slope_attn.astype(f32))
+        small_grads_ref[3:4, :] += total(slope_normed * unit_one)
+        small_grads_ref[4:5, :] += total(slope_normed)
+        small_grads_ref[5:6, :] += total(slope_outer.astype(f32))
+        small_grads_ref[6:7, :] += total(cotangent * unit_two)
+        small_grads_ref[7:8, :] += total(cotangent)
+
+    few = owners // halves
+    for half in range(halves):
+
+        @pl.when(step == tiles + half)
+        def _():
+            mine = slice(half * few * part, (half + 1) * few * part)
+
+            def put(first, count, left, right):
+                product = dot(left, right, (0, 0)).astype(bf16)
+                grads_ref[:, first : first + count, :] = product.reshape(few, count, width)
+
+            put(0, part, context_all_ref[:, mine], slope_attn_ref[...])
+            for c in range(spans):
+                span = slice(c * width, (c + 1) * width)
+                put((1 + c) * part, part, normed_ref[:, mine], slope_inner_ref[:, span])
+            deep = slice(half * few * part * spans, (half + 1) * few * part * spans)
+            put((1 + spans) * part, spans * part, active_ref[:, deep], slope_outer_ref[...])
+
+
+def middle(rows, context, cotangent, late, small, inner_shift):
+    count, width = rows.shape
+    wide = inner_shift.shape[1]
+    owners, packed, _ = late.shape
+    tiles, halves = 4, 2
+    tile = count // tiles
+    f32, bf16 = jnp.float32, jnp.bfloat16
+    token = pl.BlockSpec((tile, width), lambda i: (jnp.minimum(i, tiles - 1), 0))
+    fixed = lambda shape: pl.BlockSpec(
+        shape, lambda i: (0,) * len(shape), pipeline_mode=pl.Buffered(1)
+    )
+    whole = lambda shape: pl.BlockSpec(shape, lambda i: (0,) * len(shape))
+    return pl.pallas_call(
+        functools.partial(middle_kernel, tiles, halves),
+        grid=(tiles + halves,),
+        in_specs=[
+            token,
+            token,
+            token,
+            fixed(late.shape),
+            fixed(small.shape),
+            fixed(inner_shift.shape),
+        ],
+        out_specs=[
+            token,
+            token,
+            token,
+            pl.BlockSpec(
+                (owners // halves, packed, width), lambda i: (jnp.maximum(i - tiles, 0), 0, 0)
+            ),
+            whole((8, width)),
+            whole((1, wide)),
+        ],
+        out_shape=[
+            jax.ShapeDtypeStruct((count, width), bf16),
+            jax.ShapeDtypeStruct((count, width), f32),
+            jax.ShapeDtypeStruct((count, width), bf16),
+            jax.ShapeDtypeStruct(late.shape, bf16),
+            jax.ShapeDtypeStruct((8, width), f32),
+            jax.ShapeDtypeStruct((1, wide), f32),
+        ],
+        scratch_shapes=[
+            pltpu.VMEM((count, wide), bf16),
+            pltpu.VMEM((count, wide), bf16),
+            pltpu.VMEM((count, width), bf16),
+            pltpu.VMEM((count, width), bf16),
+            pltpu.VMEM((count, width), bf16),
+            pltpu.VMEM((count, width), bf16),
+            pltpu.VMEM((tile, wide), f32),
+        ],
+        name="middle",
+        compiler_params=pltpu.CompilerParams(vmem_limit_bytes=60 << 20),
+    )(rows, context, cotangent, late, small, inner_shift)
+
+
+def last_kernel(
+    rows_ref,
+    slope_query_ref,
+    slope_keys_ref,
+    slope_values_ref,
+    slope_first_ref,
+    early_ref,
+    hidden_grad_ref,
+    grads_ref,
+    shift_grads_ref,
+):
+    half = pl.program_id(0)
+    f32, bf16 = jnp.float32, jnp.bfloat16
+    few = grads_ref.shape[0]
+    width = rows_ref.shape[1]
+    part = part_of(early_ref)
+    tile = hidden_grad_ref.shape[0]
+    at = pl.ds(pl.multiple_of(half * tile, tile), tile)
+    mine = rows_ref[:, pl.ds(pl.multiple_of(half * few * part, few * part), few * part)]
+    grad = slope_first_ref[...]
+    for index, ref in enumerate((slope_query_ref, slope_keys_ref, slope_values_ref)):
+        weight = early_ref[:, index * part : (index + 1) * part, :].reshape(width, width)
+        grad = grad + dot(ref[at, :], weight, (1, 1))
+        grads_ref[:, index * part : (index + 1) * part, :] = (
+            dot(mine, ref[...], (0, 0)).astype(bf16).reshape(few, part, width)
+        )
+    hidden_grad_ref[...] = grad.astype(bf16)
+    grads_ref[:, 3 * part :, :] = jnp.zeros_like(grads_ref[:, 3 * part :, :])
+
+    @pl.when(half == 0)
+    def _():
+        shift_grads_ref[0:1, :] = jnp.sum(slope_query_ref[...].astype(f32), axis=0, keepdims=True)
+        shift_grads_ref[1:2, :] = jnp.sum(slope_values_ref[...].astype(f32), axis=0, keepdims=True)
+
+
+def last(rows, slope_query, slope_keys, slope_values, slope_first, early):
+    count, width = rows.shape
+    owners = early.shape[0]
+    f32, bf16 = jnp.float32, jnp.bfloat16
+    full = pl.BlockSpec((count, width), lambda i: (0, 0), pipeline_mode=pl.Buffered(1))
+    token = pl.BlockSpec((count // 2, width), lambda i: (i, 0))
+    return pl.pallas_call(
+        last_kernel,
+        grid=(2,),
+        in_specs=[full] * 4
+        + [
+            token,
+            pl.BlockSpec(early.shape, lambda i: (0, 0, 0), pipeline_mode=pl.Buffered(1)),
+        ],
+        out_specs=[
+            token,
+            pl.BlockSpec((owners // 2,) + early.shape[1:], lambda i: (i, 0, 0)),
+            pl.BlockSpec((2, width), lambda i: (0, 0)),
+        ],
+        out_shape=[
+            jax.ShapeDtypeStruct((count, width), bf16),
+            jax.ShapeDtypeStruct(early.shape, bf16),
+            jax.ShapeDtypeStruct((2, width), f32),
+        ],
+        name="last",
+    )(rows, slope_query, slope_keys, slope_values, slope_first, early)
 
 
 def to_whole_sequences(array):
@@ -466,133 +847,57 @@
     cot_all = to_whole_sequences(cotangent)
     segment_rows = lax.dynamic_slice_in_dim(segments, lax.axis_index("seq") * each, each, 0)
 
-    def square(pack, index):
-        return pack[:, index * part : (index + 1) * part].reshape(width, width)
-
-    whole_query, whole_key, whole_value = (square(early, i) for i in range(3))
     flat_small = early[:, 3 * part :].reshape(owners, small_rows * width)
     vectors = []
     at = 0
     for size in small_sizes:
-        vectors.append(flat_small[:, at : at + size].reshape(owners * size).astype(f32))
+        vectors.append(flat_small[:, at : at + size].reshape(1, owners * size).astype(f32))
         at += size
-    (
-        query_shift,
-        value_shift,
-        output_shift,
-        gain_one,
-        shift_one,
-        outer_shift,
-        gain_two,
-        shift_two,
-        inner_shift,
-    ) = vectors
-    whole_output = square(late, 0)
-    whole_inner = jnp.concatenate([square(late, 1 + c) for c in range(spans)], axis=1)
-    whole_outer = late[:, (1 + spans) * part :].reshape(wide, width)
+    small_vectors = jnp.concatenate(vectors[:-1], axis=0)
 
     length = rows_all.shape[1]
-    rows = rows_all.reshape(each * length, width)
-    grad_out = cot_all.reshape(each * length, width).astype(f32)
-
-    query = (matmul(rows, whole_query) + query_shift).astype(bf16)
-    keys = matmul(rows, whole_key).astype(bf16)
-    values = (matmul(rows, whole_value) + value_shift).astype(bf16)
-    cut = lambda array, i: array[i * length : (i + 1) * length]
-    contexts, totals = [], []
-    for i in range(each):
-        piece, total = attention_forward(
-            cut(query, i), cut(keys, i), cut(values, i), segment_rows[i], block_perm
-        )
-        contexts.append(piece)
-        totals.append(total)
-    context = jnp.concatenate(contexts, axis=0) if each > 1 else contexts[0]
-    first = rows.astype(f32) + (matmul(context, whole_output) + output_shift)
-    normed = norm_core(first, gain_one) + shift_one
-    normed_low = normed.astype(bf16)
-    inner = matmul(normed_low, whole_inner) + inner_shift
-    active = exact_gelu(inner).astype(bf16)
-    second = normed + (matmul(active, whole_outer) + outer_shift)
-    result = norm_core(second, gain_two) + shift_two
-    layer_out = to_token_shards(result.astype(bf16).reshape(each, length, width))
-
-    _, second_back = jax.vjp(norm_core, second, gain_two)
-    slope_second, grad_gain_two = second_back(grad_out)
-    grad_shift_two = jnp.sum(grad_out, axis=0)
-    slope_outer = slope_second.astype(bf16)
-    grad_outer_shift = column_sum(slope_outer)
-    grad_outer = transposed_times(active, slope_outer)
-    _, gelu_back = jax.vjp(exact_gelu, inner)
-    slope_inner = gelu_back(times_transposed(slope_outer, whole_outer))[0].astype(bf16)
-    grad_inner_shift = column_sum(slope_inner)
-    grad_inner = transposed_times(normed_low, slope_inner)
-    late_grads = jnp.concatenate(
-        [grad_inner[:, c * width : (c + 1) * width].astype(bf16).reshape(owners, part, width) for c in range(spans)]
-        + [grad_outer.astype(bf16).reshape(owners, spans * part, width)],
-        axis=1,
-    )
+    rows = rows_all.reshape(length, width)
+    segment_row = segment_rows.reshape(length)
+    query, keys, values = project(rows, early, small_vectors)
+    (context,) = attend_call(
+        attend_kernel, (query, keys, values), segment_row, block_perm, 1, "attend"
+    )
+    result, slope_first, slope_context, late_grads, small_grads, inner_shift_grad = middle(
+        rows, context, cot_all.reshape(length, width), late, small_vectors, vectors[-1]
+    )
+    layer_out = to_token_shards(result.reshape(each, length, width))
     late_owned = lax.psum_scatter(late_grads, "fsdp", scatter_dimension=0, tiled=False)
-    slope_normed = slope_second + times_transposed(slope_inner, whole_inner)
-    _, first_back = jax.vjp(norm_core, first, gain_one)
-    slope_first, grad_gain_one = first_back(slope_normed)
-    grad_shift_one = jnp.sum(slope_normed, axis=0)
-    slope_attn = slope_first.astype(bf16)
-    grad_output_shift = column_sum(slope_attn)
-    grad_output = transposed_times(context, slope_attn)
-    slope_context = times_transposed(slope_attn, whole_output).astype(bf16)
-    slopes = [
-        attention_backward(
-            cut(query, i),
-            cut(keys, i),
-            cut(values, i),
-            cut(slope_context, i),
-            segment_rows[i],
-            block_perm,
-            totals[i],
-        )
-        for i in range(each)
-    ]
-    slope_query, slope_keys, slope_values = (
-        jnp.concatenate(parts, axis=0) if each > 1 else parts[0] for parts in zip(*slopes)
-    )
-    slope_rows = (
-        slope_first
-        + times_transposed(slope_query, whole_query)
-        + times_transposed(slope_keys, whole_key)
-        + times_transposed(slope_values, whole_value)
-    )
-    hidden_grad = to_token_shards(slope_rows.astype(bf16).reshape(each, length, width))
-    grad_query = transposed_times(rows, slope_query)
-    grad_query_shift = column_sum(slope_query)
-    grad_key = transposed_times(rows, slope_keys)
-    grad_value = transposed_times(rows, slope_values)
-    grad_value_shift = column_sum(slope_values)
-    small_grads = (
-        grad_query_shift,
-        grad_value_shift,
-        grad_output_shift,
-        grad_gain_one,
-        grad_shift_one,
-        grad_outer_shift,
-        grad_gain_two,
-        grad_shift_two,
-        grad_inner_shift,
-    )
-    slab = lambda array: array.astype(bf16).reshape(owners, part, width)
-    early_grads = jnp.concatenate(
-        [slab(grad_query), slab(grad_key), slab(grad_value), slab(grad_output)]
-        + [
-            small_block(
-                [piece.astype(bf16).reshape(owners, -1) for piece in small_grads], (owners,)
-            )
+    slope_query, slope_keys, slope_values = attend_call(
+        attend_back_kernel,
+        (query, keys, values, slope_context),
+        segment_row,
+        block_perm,
+        3,
+        "attend_back",
+    )
+    slope_rows, early_grads, shift_grads = last(
+        rows, slope_query, slope_keys, slope_values, slope_first, early
+    )
+    hidden_grad = to_token_shards(slope_rows.reshape(each, length, width))
+    small_grads = jnp.concatenate(
+        [
+            jnp.concatenate([shift_grads, small_grads[2:]], axis=0)
+            .reshape(-1, owners, part)
+            .swapaxes(0, 1)
+            .reshape(owners, -1),
+            inner_shift_grad.reshape(owners, -1),
         ],
         axis=1,
-    )
+    ).astype(bf16)
+    early_grads = lax.dynamic_update_slice(
+        early_grads, small_block([small_grads], (owners,)), (0, 3 * part, 0)
+    )
+    early_grads, late_owned = lax.optimization_barrier((early_grads, late_owned))
     early_owned = lax.psum_scatter(early_grads, "fsdp", scatter_dimension=0, tiled=False)
     late_owned = sum_over_seq(late_owned).astype(f32)
     early_owned = sum_over_seq(early_owned).astype(f32)
     own = lambda pack, index: pack[index * part : (index + 1) * part]
-    small_flat = early_owned[4 * part :].reshape(small_rows * width)
+    small_flat = early_owned[3 * part :].reshape(small_rows * width)
     got = []
     at = 0
     for size in small_sizes:
@@ -609,8 +914,8 @@
         own_shift_two,
         own_inner_shift,
     ) = got
-    own_inner = jnp.concatenate([own(late_owned, c) for c in range(spans)], axis=1)
-    own_outer = late_owned[spans * part :]
+    own_inner = jnp.concatenate([own(late_owned, 1 + c) for c in range(spans)], axis=1)
+    own_outer = late_owned[(1 + spans) * part :]
     return (
         layer_out,
         hidden_grad,
@@ -619,7 +924,7 @@
         own(early_owned, 1),
         own(early_owned, 2),
         own_value_shift,
-        own(early_owned, 3),
+        own(late_owned, 0),
         own_output_shift,
         own_gain_one,
         own_shift_one,
@@ -633,7 +938,7 @@
 
 
 def on_device(hidden, *rest):
-    if hidden.shape[0] % lax.axis_size("seq") == 0:
+    if hidden.shape[0] == lax.axis_size("seq"):
         return on_device_whole(hidden, *rest)
     return on_device_general(hidden, *rest)
 

time: 564 us -> 443 us (0.79)
  matrix products: 169 us -> 0 us
  Pallas kernels: 0 us -> 137 us
  local copies, waits for them, and re-layouts: 115 us -> 42.2 us
  other arithmetic: 78.8 us -> 29.6 us
  blocking collectives: 0 us -> 24 us
  waiting for transfers between devices: 162 us -> 175 us
  starting transfers between devices: 21.9 us -> 15.5 us
    dot_general x30 -> x0, matrix products: 169 us -> none  [the longest x6 68.8 us: matmul(): return jnp.dot(left, right, preferred_element_type=jnp.float32)]
    pallas_call x0 -> x5, Pallas kernels: none -> 137 us  [the longest x1 63.9 us: middle(): pl.pallas_call(functools.partial(middle_kernel, tiles, halves), grid=(til...]
    all_gather x1, waiting for transfers between devices: 21 us -> 59.3 us  [on_device_whole(): late = lax.all_gather(late_pack, 'fsdp', axis=0, tiled=False)]
    all_to_all x2 -> x1, waiting for transfers between devices: 33.2 us -> 0.01 us  [to_whole_sequences(): return lax.all_to_all(array, 'seq', split_axis=0, concat_axis=1, tiled=True)]
    reduce_sum x12 -> x0, other arithmetic: 28.3 us -> none  [the longest x4 13.1 us: column_sum(): return jnp.sum(values.astype(jnp.float32), axis=0)]
    unnamed x180 -> x31, local copies, waits for them, and re-layouts: 45.8 us -> 19.5 us
    all_to_all x0 -> x1, blocking collectives: none -> 24 us  [to_whole_sequences(): return lax.all_to_all(array, 'seq', split_axis=0, concat_axis=1, tiled=True)]
    convert_element_type x4 -> x1, other arithmetic: 18.4 us -> 0.01 us  [on_device_whole(): flat_small[:, at:at + size].reshape(1, owners * size).astype(f32)]
  transfers between devices with their start and end apart: 10 -> 9, of which waited for: 6 -> 7; matrix products, arithmetic and copies ran while one was open for 27% -> 14% of each run, Pallas kernels for 0% -> 17%
where the time goes in v2:
time: 443 us; the launch traced here: 438 us
  waiting for transfers between devices  175 us (40%)
  Pallas kernels  137 us (31%)
  local copies, waits for them, and re-layouts  42.2 us (10%)
  other arithmetic  29.6 us (7%)
  blocking collectives  24 us (5%)
  starting transfers between devices  15.5 us (3%)
  between operations  14.2 us (3%)
    reduce_scatter x1, waiting for transfers between devices, on_device_whole(): lax.psum_scatter(late_grads, 'fsdp', scatter_dimension=0, tiled=False)  70.5 us
    pallas_call x1, Pallas kernels, middle(): pl.pallas_call(functools.partial(middle_kernel, tiles, halves), grid=(til...  63.9 us
    all_gather x1, waiting for transfers between devices, on_device_whole(): late = lax.all_gather(late_pack, 'fsdp', axis=0, tiled=False)  59.3 us
    pallas_call x2, Pallas kernels, attend_call(): pl.pallas_call(kernel, grid_spec=pltpu.PrefetchScalarGridSpec(num_scalar_...  51.6 us
    all_to_all x1, blocking collectives, to_whole_sequences(): return lax.all_to_all(array, 'seq', split_axis=0, concat_axis=1, tiled=True)  24 us
    unnamed x2, other arithmetic  23.4 us
    unnamed x31, local copies, waits for them, and re-layouts  19.5 us
    all_gather x1, waiting for transfers between devices, on_device_whole(): early = lax.all_gather(early_pack, 'fsdp', axis=0, tiled=False)  16.2 us
  transfers between devices with their start and end apart: 9, of which 7 were waited for; matrix products, arithmetic and copies ran while one was open for 14% of the time, Pallas kernels for 17%

profile of v2, /device:TPU:0, one launch (start us, length us, event | category | flops | bytes accessed | tf_op | source)
XLA Modules:
  0.0 438.1 jit_solution(14889996444329501797)
XLA Ops:
  7.3 6.2 %concatenate.25 = bf16[576]{0:T(1024)(128)(2,1)S(1)} concatenate(bf16[48]{0:T(256)(128)(2,1)} %param.23, bf16[48]{0:T(256)(128)(2,1)} %param.26, bf16[48]{0:T(256)(128)(2,1)} %param.28, bf16[48]{0:T(256)(128)(2,1)} %param.29, bf16[48]{0:T(256)(128)(2,1)} %param.30, bf16[48]{0:T(256)(128)(2,1)} %param.34, bf16[48]{0:T(256)(128)(2,1)} %param.35, bf16[48]{0:T(256)(128)(2,1)} %param.36, ...), dimensions={0} | concatenate | bytes 2304 | tf_op jit(solution)/shard_map/concatenate | solution.py:830
  13.5 1.7 pad_maximum_fusion.1
  20.7 24.0 %all_to_all.42 = bf16[2,512,768]{2,1,0:T(8,128)(2,1)} all-to-all(bf16[2,512,768]{2,1,0:T(8,128)(2,1)S(1)} %copy-done.1), channel_id=1, replica_groups=mesh['fsdp'=16,'seq'=2] {'seq'}, dimensions={0} | all-to-all | bytes 3145728 | tf_op jit(solution)/shard_map/all_to_all | solution.py:771
  44.7 3.8 all-to-all-start.1
  48.6 1.0 copy.52.segment_column_ref
  50.9 16.2 %all-gather.5.cloned.1.call-done = bf16[2560,768]{1,0:T(8,128)(2,1)} async-done(((bf16[160,768]{1,0:T(8,128)(2,1)}), bf16[2560,768]{1,0:T(8,128)(2,1)}) %all-gather.5.cloned.1.call-update) | async-done | bytes 3932176 | tf_op jit(solution)/shard_map/all_gather | solution.py:843
  67.1 1.0 slice.137
  70.5 7.3 %project.1 = (bf16[1024,768]{1,0:T(8,128)(2,1)}, bf16[1024,768]{1,0:T(8,128)(2,1)}, bf16[1024,768]{1,0:T(8,128)(2,1)}) custom-call(bf16[1024,768]{1,0:T(8,128)(2,1)} %bitcast.26, bf16[16,160,768]{2,1,0:T(8,128)(2,1)} %bitcast.30, f32[8,768]{1,0:T(8,128)} %concatenate.28.small_ref), custom_call_target="tpu_custom_call" | custom-call | tf_op jit(solution)/shard_map/project/pallas_call | solution.py:410
  77.8 19.3 %attend.1.context_ref = bf16[1024,768]{1,0:T(8,128)(2,1)} custom-call(s32[12,2]{1,0:T(8,128)} %copy.51.perm_ref, bf16[1024,768]{1,0:T(8,128)(2,1)} %get-tuple-element.34.query_ref, bf16[1024,768]{1,0:T(8,128)(2,1)} %get-tuple-element.35.keys_ref, bf16[1024,768]{1,0:T(8,128)(2,1)} %get-tuple-element.36.values_ref, s32[2,512]{1,0:T(2,128)} %reshape_reshape.8.segment_row_ref, ...), custom_call_target="tpu_custom_call" | custom-call | tf_op jit(solution)/shard_map/attend/pallas_call | solution.py:501
  97.1 59.3 %all-gather.7.cloned.1.call-done = bf16[6912,768]{1,0:T(8,128)(2,1)} async-done(((bf16[432,768]{1,0:T(8,128)(2,1)}), bf16[6912,768]{1,0:T(8,128)(2,1)}) %all-gather.7.cloned.1.call-update) | async-done | bytes 10616848 | tf_op jit(solution)/shard_map/all_gather | solution.py:844
  156.4 63.9 %middle.1 = (bf16[1024,768]{1,0:T(8,128)(2,1)}, f32[1024,768]{1,0:T(8,128)}, bf16[1024,768]{1,0:T(8,128)(2,1)}, bf16[16,432,768]{2,1,0:T(8,128)(2,1)}, f32[8,768]{1,0:T(8,128)}, /*index=5*/f32[1,3072]{1,0:T(1,128)}) custom-call(bf16[1024,768]{1,0:T(8,128)(2,1)} %bitcast.27, bf16[1024,768]{1,0:T(8,128)(2,1)} %attend.1.context_ref, ...), custom_call_target="tpu_custom_call" | custom-call | tf_op jit(solution)/shard_map/middle/pallas_call | solution.py:664
  220.4 32.3 %attend_back.1 = (bf16[1024,768]{1,0:T(8,128)(2,1)}, bf16[1024,768]{1,0:T(8,128)(2,1)}, bf16[1024,768]{1,0:T(8,128)(2,1)}) custom-call(s32[12,2]{1,0:T(8,128)} %copy.51.perm_ref, bf16[1024,768]{1,0:T(8,128)(2,1)} %get-tuple-element.34.query_ref, bf16[1024,768]{1,0:T(8,128)(2,1)} %get-tuple-element.35.keys_ref, ...), custom_call_target="tpu_custom_call" | custom-call | tf_op jit(solution)/shard_map/attend_back/pallas_call | solution.py:501
  252.6 14.3 %last.1 = (bf16[1024,768]{1,0:T(8,128)(2,1)}, bf16[16,160,768]{2,1,0:T(8,128)(2,1)}, f32[2,768]{1,0:T(2,128)}) custom-call(bf16[1024,768]{1,0:T(8,128)(2,1)} %bitcast.28, bf16[1024,768]{1,0:T(8,128)(2,1)} %get-tuple-element.39.slope_query_ref, bf16[1024,768]{1,0:T(8,128)(2,1)} %get-tuple-element.40.slope_keys_ref, ...), custom_call_target="tpu_custom_call" | custom-call | tf_op jit(solution)/shard_map/last/pallas_call | solution.py:748
  268.9 70.5 %reduce-scatter.3.cloned.1.call-done = bf16[1,432,768]{2,1,0:T(8,128)(2,1)} async-done(((bf16[16,432,768]{2,1,0:T(8,128)(2,1)}), bf16[1,432,768]{2,1,0:T(8,128)(2,1)}) %reduce-scatter.3.cloned.1.call-update) | async-done | bytes 663568 | tf_op jit(solution)/shard_map/reduce_scatter | solution.py:869
  339.4 3.8 copy.64
  343.8 11.8 %reduce.7 = bf16[1024,768]{1,0:T(8,128)(2,1)} reduce(bf16[1024,1,768]{2,1,0:T(2,128)(2,1)S(1)} %bitcast.32, bf16[]{:T(256)} %broadcast.14), dimensions={1}, to_apply=%bitcast.24.reduce_sub_computation | reduce | bytes 3145730
  355.5 2.5 reshape.243
  358.1 4.7 %all-to-all-start.3 = ((bf16[2,2,196608]{2,1,0:T(2,128)(2,1)}), bf16[2,2,196608]{2,1,0:T(2,128)(2,1)}, u32[]{:S(2)}, u32[]{:S(2)}) async-start(bf16[2,2,196608]{2,1,0:T(2,128)(2,1)} %reshape.243), calls=%async_computation.3 | async-start | bytes 3145728 | tf_op jit(solution)/shard_map/all_to_all | solution.py:775
  362.7 3.8 copy.65
  366.6 11.6 %reduce.6 = bf16[1024,768]{1,0:T(8,128)(2,1)} reduce(bf16[1024,1,768]{2,1,0:T(2,128)(2,1)S(1)} %bitcast.33, bf16[]{:T(256)} %broadcast.14), dimensions={1}, to_apply=%bitcast.25.reduce_sub_computation | reduce | bytes 3145730
  378.2 2.5 reshape.241
  380.6 1.3 all-to-all-done.3
  381.9 4.6 %all-to-all-start.2 = ((bf16[2,2,196608]{2,1,0:T(2,128)(2,1)}), bf16[2,2,196608]{2,1,0:T(2,128)(2,1)}, u32[]{:S(2)}, u32[]{:S(2)}) async-start(bf16[2,2,196608]{2,1,0:T(2,128)(2,1)} %reshape.241), calls=%async_computation.2 | async-start | bytes 3145728 | tf_op jit(solution)/shard_map/all_to_all | solution.py:775
  386.5 2.0 collective-permute-start.1
  388.5 2.5 reshape.244
  391.0 1.4 copy.59
  392.4 14.8 %all-to-all-done.2 = bf16[2,2,196608]{2,1,0:T(2,128)(2,1)} async-done(((bf16[2,2,196608]{2,1,0:T(2,128)(2,1)}), bf16[2,2,196608]{2,1,0:T(2,128)(2,1)}, u32[]{:S(2)}, u32[]{:S(2)}) %all-to-all-start.2) | async-done | bytes 1572896 | tf_op jit(solution)/shard_map/all_to_all | solution.py:775
  407.2 2.5 reshape.242
  409.7 1.4 copy.58
  411.1 7.9 %collective-permute-done.1 = bf16[432,768]{1,0:T(8,128)(2,1)} collective-permute-done((bf16[432,768]{1,0:T(8,128)(2,1)}, bf16[432,768]{1,0:T(8,128)(2,1)}, u32[]{:S(2)}, u32[]{:S(2)}) %collective-permute-start.1) | collective-permute-done | bytes 663584 | tf_op jit(solution)/shard_map/ppermute | solution.py:780
  419.0 1.4 add_convert_fusion
  423.2 5.3 %collective-permute-done = bf16[160,768]{1,0:T(8,128)(2,1)S(1)} collective-permute-done((bf16[160,768]{1,0:T(8,128)(2,1)}, bf16[160,768]{1,0:T(8,128)(2,1)S(1)}, u32[]{:S(2)}, u32[]{:S(2)}) %collective-permute-start) | collective-permute-done | bytes 245792 | tf_op jit(solution)/shard_map/ppermute | solution.py:780
  (73 shorter events, 17.3 us)
Async XLA Ops:
  7.2 12.5 %copy-start.3 = (bf16[192,768]{1,0:T(8,128)(2,1)S(1)}, bf16[192,768]{1,0:T(8,128)(2,1)}, u32[]{:S(2)}) copy-start(bf16[192,768]{1,0:T(8,128)(2,1)} %param.33) | copy-start | bytes 884740
  7.2 13.5 %copy-start.1 = (bf16[2,512,768]{2,1,0:T(8,128)(2,1)S(1)}, bf16[2,512,768]{2,1,0:T(8,128)(2,1)}, u32[]{:S(2)}) copy-start(bf16[2,512,768]{2,1,0:T(8,128)(2,1)} %param.19) | copy-start | bytes 4718596
  7.2 59.9 %all-gather.5.cloned.1.call-start = ((), (), s32[]{:S(2)}) async-start(), calls=%async_computation.8 | async-start | bytes 4177920 | tf_op jit(solution)/shard_map/all_gather | solution.py:843
  15.2 141.2 %all-gather.7.cloned.1.call-start = ((), (), s32[]{:S(2)}) async-start(), calls=%async_computation.9 | async-start | bytes 11280384 | tf_op jit(solution)/shard_map/all_gather | solution.py:844
  19.7 0.9 copy-start.2
  44.7 3.9 copy-start.6
  44.7 5.5 %copy-start.7 = (s32[12,2]{0,1:T(2,128)S(1)}, s32[12,2]{0,1:T(2,128)}, u32[]{:S(2)}) copy-start(s32[12,2]{0,1:T(2,128)} %param.21) | copy-start | bytes 292
  44.7 52.4 %all-to-all-start.1 = ((bf16[2,512,768]{2,1,0:T(8,128)(2,1)}), bf16[2,512,768]{2,1,0:T(8,128)(2,1)S(1)}, u32[]{:S(2)}, u32[]{:S(2)}) async-start(bf16[2,512,768]{2,1,0:T(8,128)(2,1)} %param.37), calls=%async_computation.1 | async-start | bytes 3145728 | tf_op jit(solution)/shard_map/all_to_all | solution.py:771
  48.5 290.9 %reduce-scatter.3.cloned.1.call-start = ((), (), s32[]{:S(2)}) async-start(), calls=%async_computation.6 | async-start | bytes 11280384 | tf_op jit(solution)/shard_map/reduce_scatter | solution.py:869
  97.1 59.3 %copy-start = (bf16[2,512,768]{2,1,0:T(8,128)(2,1)}, bf16[2,512,768]{2,1,0:T(8,128)(2,1)S(1)}, u32[]{:S(2)}) copy-start(bf16[2,512,768]{2,1,0:T(8,128)(2,1)S(1)} %all-to-all-done.1) | copy-start | bytes 4718596
  220.3 201.7 %reduce-scatter.5.cloned.1.call-start = ((), (), s32[]{:S(2)}) async-start(), calls=%async_computation.7 | async-start | bytes 4177920 | tf_op jit(solution)/shard_map/reduce_scatter | solution.py:896
  252.6 15.0 %copy-start.5 = (f32[8,768]{1,0:T(8,128)S(1)}, f32[8,768]{1,0:T(8,128)}, u32[]{:S(2)}) copy-start(f32[8,768]{1,0:T(8,128)} %get-tuple-element.46) | copy-start | bytes 73732
  252.6 15.2 %copy-start.4 = (f32[1,3072]{1,0:T(1,128)S(1)}, f32[1,3072]{1,0:T(1,128)}, u32[]{:S(2)}) copy-start(f32[1,3072]{1,0:T(1,128)} %get-tuple-element.47) | copy-start | bytes 36868
  358.1 23.8 %all-to-all-start.3 = ((bf16[2,2,196608]{2,1,0:T(2,128)(2,1)}), bf16[2,2,196608]{2,1,0:T(2,128)(2,1)}, u32[]{:S(2)}, u32[]{:S(2)}) async-start(bf16[2,2,196608]{2,1,0:T(2,128)(2,1)} %reshape.243), calls=%async_computation.3 | async-start | bytes 3145728 | tf_op jit(solution)/shard_map/all_to_all | solution.py:775
  381.9 25.3 %all-to-all-start.2 = ((bf16[2,2,196608]{2,1,0:T(2,128)(2,1)}), bf16[2,2,196608]{2,1,0:T(2,128)(2,1)}, u32[]{:S(2)}, u32[]{:S(2)}) async-start(bf16[2,2,196608]{2,1,0:T(2,128)(2,1)} %reshape.241), calls=%async_computation.2 | async-start | bytes 3145728 | tf_op jit(solution)/shard_map/all_to_all | solution.py:775
  386.5 32.5 %collective-permute-start.1 = (bf16[432,768]{1,0:T(8,128)(2,1)}, bf16[432,768]{1,0:T(8,128)(2,1)}, u32[]{:S(2)}, u32[]{:S(2)}) collective-permute-start(bf16[432,768]{1,0:T(8,128)(2,1)} %bitcast.8), channel_id=1, source_target_pairs={{0,1},{1,0},{2,3},{3,2},{4,5},{5,4},{6,7},{7,6},{8,9},{9,8},{10,11... | collective-permute-start | bytes 1990664 | tf_op jit(solution)/shard_map/ppermute | solution.py:780
  422.0 6.4 %collective-permute-start = (bf16[160,768]{1,0:T(8,128)(2,1)}, bf16[160,768]{1,0:T(8,128)(2,1)S(1)}, u32[]{:S(2)}, u32[]{:S(2)}) collective-permute-start(bf16[160,768]{1,0:T(8,128)(2,1)} %bitcast.47), channel_id=1, source_target_pairs={{0,1},{1,0},{2,3},{3,2},{4,5},{5,4},{6,7},{7,6},{8,9},{9,8},{10,11... | collective-permute-start | bytes 737288 | tf_op jit(solution)/shard_map/ppermute | solution.py:780
Sparse Core Ops, SparseCore 0:
  15.3 51.7 all-gather.4
  69.4 86.9 all-gather.6
  220.4 118.8 reduce-scatter.2
  343.1 70.0 reduce-scatter.4
